TPU v7x, 32 devices: a whole 2x2x4 slice. The times are simulated.
32 devices in a mesh: groups: 2 (over y), blk: 4 (over z), rep: 4 (over x, core).
Axes of the slice: x: 2, y: 2, z: 4, core: 2. Of those that a mesh axis runs over, the one named last changes fastest.
Arguments:
- orbitals: float32 [8, 262144], P(('groups', 'blk')), parts along dimension 0, may hold values from -6 to 6
- offsets: int32 [8], P('groups'), parts along dimension 0, may hold values from 0 to 3
Outputs:
- exchanged: float32 [8, 262144], P(('groups', 'blk'), 'rep'), parts along dimension 0
- margin: float32 [8, 4], P(('groups', 'blk')), parts along dimension 0
There are 2 independent parts, one for each index of `groups`. A program takes and returns all parts, laid end to end along the dimension named above; each array names one. Nothing has to cross between parts.
All inputs are finite; a program needn't handle non-finite values.
Results may differ from a plain program's by a relative error of at most 0.0001.
Values sent between devices are 32-bit elements; how exact they have to be, the bound alone decides.
A program may use at most 64 MiB of HBM per device.

v0:
```python
import jax
import jax.numpy as jnp
from jax import lax
from jax.sharding import PartitionSpec as P

NG = 64


precise_mode = lax.Precision.HIGHEST
screen_scale = 0.05


def passed_along(block, axis, distance):
    devices = range(lax.axis_size(axis))
    route = [((i - distance) % len(devices), i) for i in devices]
    return lax.ppermute(block, axis, route)


def cas_table(grid_points):
    grid_index = jnp.arange(grid_points, dtype=jnp.int32)
    product = grid_index[:, None] * grid_index[None, :] % grid_points
    phase_angle = 2.0 * jnp.pi / grid_points * product.astype(jnp.float32)
    return jnp.cos(phase_angle) + jnp.sin(phase_angle)


def screened_kernel(grid_points):
    grid_index = jnp.arange(grid_points, dtype=jnp.int32)
    folded = jnp.where(grid_index <= grid_points // 2, grid_index, grid_index - grid_points).astype(
        jnp.float32
    )
    squares = folded * folded
    k_squared = squares[:, None, None] + squares[None, :, None] + squares[None, None, :]
    safe_square = jnp.maximum(k_squared, 1.0)
    screened = (
        4.0
        * jnp.pi
        / (screen_scale * safe_square)
        * (1.0 - jnp.exp(-screen_scale * safe_square / (4.0 * jnp.pi)))
    )
    return jnp.where(k_squared > 0.5, screened, jnp.ones_like(screened))


def transform(values_field, cas_values, cas_paired):
    batch_size = values_field.shape[0]
    grid_points = values_field.shape[1]
    values_field = jnp.einsum(
        "kx,pxq->pkq",
        cas_values,
        values_field.reshape(batch_size, grid_points, grid_points * grid_points),
        precision=precise_mode,
    )
    values_field = jnp.einsum(
        "ky,ayz->akz",
        cas_values,
        values_field.reshape(batch_size * grid_points, grid_points, grid_points),
        precision=precise_mode,
    )
    values_field = jnp.dot(
        values_field.reshape(batch_size * grid_points * grid_points // 2, 2 * grid_points),
        cas_paired,
        precision=precise_mode,
    )
    return values_field.reshape(batch_size, grid_points, grid_points, grid_points)


def cycle_term(own_block, visiting, cas_values, cas_paired, kernel):
    grid_points = kernel.shape[0]
    block_rows = own_block.shape[0]
    density = (own_block[:, None, :] * visiting[None, :, :]).reshape(
        block_rows * block_rows, grid_points, grid_points, grid_points
    )
    spectrum = transform(density, cas_values, cas_paired) * kernel[None]
    potential = transform(spectrum, cas_values, cas_paired).reshape(
        block_rows, block_rows, grid_points**3
    ) / float(grid_points**3)
    return jnp.sum(potential * visiting[None, :, :], axis=1)


def position_block(orbital_block, amount):
    bit_count = (lax.axis_size("blk") - 1).bit_length()
    for bit_level in range(bit_count):
        moved_block = passed_along(orbital_block, "blk", 1 << bit_level)
        orbital_block = jnp.where(amount // (1 << bit_level) % 2 == 1, moved_block, orbital_block)
    return orbital_block


def local(orbitals, offsets):
    cas_values = cas_table(NG)
    cas_paired = jnp.kron(jnp.eye(2, dtype=jnp.float32), cas_values)
    kernel = screened_kernel(NG)
    cycle_size = lax.axis_size("blk")
    replica = lax.axis_index("rep")
    start_block = offsets[replica]
    first_visit = position_block(orbitals, (start_block + 1) % cycle_size)
    behind = passed_along(first_visit, "blk", -1)
    accumulator = cycle_term(orbitals, first_visit, cas_values, cas_paired, kernel)
    ahead_block = first_visit
    ahead_block = passed_along(ahead_block, "blk", 1)
    accumulator = accumulator + cycle_term(orbitals, ahead_block, cas_values, cas_paired, kernel)
    accumulator = accumulator + cycle_term(orbitals, behind, cas_values, cas_paired, kernel)
    exchanged = lax.psum_scatter(accumulator, "rep", scatter_dimension=1, tiled=True)
    quarter_cells = exchanged.shape[1]
    quarter = lax.dynamic_slice_in_dim(orbitals, replica * quarter_cells, quarter_cells, 1)
    slab_orbitals, slab_exchanged = (
        lax.all_to_all(quarter, "blk", split_axis=1, concat_axis=0, tiled=True),
        lax.all_to_all(exchanged, "blk", split_axis=1, concat_axis=0, tiled=True),
    )
    partial_value = lax.dot_general(
        slab_orbitals, slab_exchanged, (((1,), (1,)), ((), ())), precision=precise_mode
    ) / float(NG**3)
    gram_rows = lax.psum_scatter(partial_value, "blk", scatter_dimension=0, tiled=True)
    margin = lax.psum(gram_rows, "rep")
    return (exchanged, margin)


def solution(mesh):
    placed = (P(("groups", "blk"), None), P("groups"))
    return jax.shard_map(
        local,
        mesh=mesh,
        in_specs=placed,
        out_specs=(P(("groups", "blk"), "rep"), P(("groups", "blk"), None)),
        check_vma=False,
    )
```

profile of v0, /device:TPU:0, one launch (start us, length us, event | category | flops | bytes accessed | tf_op | source)
XLA Modules:
  0.0 327.6 jit_solution(143955642018694958)
XLA Ops:
  7.2 3.1 collective-permute-start
  12.2 23.5 %collective-permute-done = f32[1,262144]{1,0:T(1,128)S(1)} collective-permute-done((f32[1,262144]{1,0:T(1,128)}, f32[1,262144]{1,0:T(1,128)S(1)}, u32[]{:S(2)}, u32[]{:S(2)}) %collective-permute-start) | collective-permute-done | bytes 1048608 | tf_op jit(solution)/shard_map/ppermute | solution.py:16
  37.6 45.8 %collective-permute-done.1 = f32[1,262144]{1,0:T(1,128)S(1)} collective-permute-done((f32[1,262144]{1,0:T(1,128)S(1)}, f32[1,262144]{1,0:T(1,128)S(1)}, u32[]{:S(2)}, u32[]{:S(2)}) %collective-permute-start.1) | collective-permute-done | bytes 1048608 | tf_op jit(solution)/shard_map/ppermute | solution.py:16
  84.6 3.8 %collective-permute-start.3 = (f32[1,262144]{1,0:T(1,128)S(1)}, f32[1,262144]{1,0:T(1,128)}, u32[]{:S(2)}, u32[]{:S(2)}) collective-permute-start(f32[1,262144]{1,0:T(1,128)S(1)} %broadcast_select_fusion.1), channel_id=1, source_target_pairs={{4,0},{8,4},{12,8},{0,12},{5,1},{9,5},{13,9},{1,13},{6,2},{10,6},{... | collective-permute-start | bytes 3145736 | tf_op jit(solution)/shard_map/ppermute | solution.py:16
  91.3 21.4 %collective-permute-done.2 = f32[1,262144]{1,0:T(1,128)} collective-permute-done((f32[1,262144]{1,0:T(1,128)S(1)}, f32[1,262144]{1,0:T(1,128)}, u32[]{:S(2)}, u32[]{:S(2)}) %collective-permute-start.2) | collective-permute-done | bytes 1048608 | tf_op jit(solution)/shard_map/ppermute | solution.py:16
  112.6 19.7 %collective-permute-done.3 = f32[1,262144]{1,0:T(1,128)} collective-permute-done((f32[1,262144]{1,0:T(1,128)S(1)}, f32[1,262144]{1,0:T(1,128)}, u32[]{:S(2)}, u32[]{:S(2)}) %collective-permute-start.3) | collective-permute-done | bytes 1048608 | tf_op jit(solution)/shard_map/ppermute | solution.py:16
  132.4 14.2 %multiply_reduce_fusion.2 = (f32[262144]{0:T(1024)}, f32[262144]{0:T(1024)S(1)}, f32[262144]{0:T(1024)}) fusion(f32[1,262144]{1,0:T(1,128)} %param.2, f32[1,262144]{1,0:T(1,128)S(1)} %broadcast_select_fusion.1, f32[1,262144]{1,0:T(1,128)} %collective-permute-done.2, f32[1,262144]{1,0:T(1,128)} %collective-permute-done.3), kind=kLoop, calls=%fused_computation.25 | loop fusion | flops 786432 | bytes 7340032 | tf_op jit(solution)/shard_map/mul | solution.py:69
  151.0 4.8 %convolution_bitcast_fusion.9 = f32[64,64,64]{1,2,0:T(8,128)} fusion(f32[64,64,64]{2,1,0:T(8,128)S(1)} %reshape.337), kind=kOutput, calls=%fused_computation.14 | convolution fusion | flops 201388032 | bytes 2097152 | tf_op jit(solution)/shard_map/ky,ayz->akz/dot_general | solution.py:52
  159.2 2.3 fusion.70
  162.7 3.9 %convolution_bitcast_fusion.2 = f32[1,64,4096]{2,1,0:T(8,128)} fusion(f32[64,4096]{1,0:T(8,128)} %reshape.339, f32[64,4096]{1,0:T(8,128)S(1)} %copy-done.4, f32[4096]{0:T(1024)S(1)} %add.227), kind=kOutput, calls=%fused_computation.2 | convolution fusion | flops 204009472 | bytes 3162112 | tf_op jit(solution)/shard_map/kx,pxq->pkq/dot_general | solution.py:46
  168.6 4.8 %convolution_bitcast_fusion.8 = f32[64,64,64]{1,2,0:T(8,128)} fusion(f32[64,64,64]{2,1,0:T(8,128)S(1)} %reshape.340), kind=kOutput, calls=%fused_computation.13 | convolution fusion | flops 201388032 | bytes 2097152 | tf_op jit(solution)/shard_map/ky,ayz->akz/dot_general | solution.py:52
  176.6 3.3 %convolution_multiply_fusion.1 = f32[2048,128]{1,0:T(8,128)} fusion(f32[2048,128]{1,0:T(8,128)} %reshape.341, f32[128,128]{1,0:T(8,128)S(1)} %mul.403), kind=kOutput, calls=%fused_computation.7 | convolution fusion | flops 402915328 | bytes 2162688 | tf_op jit(solution)/shard_map/dot_general | solution.py:58
  182.2 2.2 reshape.332
  184.5 4.8 %convolution_bitcast_fusion.11 = f32[64,64,64]{1,2,0:T(8,128)} fusion(f32[64,64,64]{2,1,0:T(8,128)S(1)} %reshape.332), kind=kOutput, calls=%fused_computation.16 | convolution fusion | flops 201388032 | bytes 2097152 | tf_op jit(solution)/shard_map/ky,ayz->akz/dot_general | solution.py:52
  192.5 2.3 fusion.69
  195.9 3.9 %convolution_bitcast_fusion.4 = f32[1,64,4096]{2,1,0:T(8,128)} fusion(f32[64,4096]{1,0:T(8,128)} %reshape.334, f32[64,4096]{1,0:T(8,128)S(1)} %copy-done.5, f32[4096]{0:T(1024)S(1)} %add.227), kind=kOutput, calls=%fused_computation.4 | convolution fusion | flops 204009472 | bytes 3162112 | tf_op jit(solution)/shard_map/kx,pxq->pkq/dot_general | solution.py:46
  201.9 4.8 %convolution_bitcast_fusion.10 = f32[64,64,64]{1,2,0:T(8,128)} fusion(f32[64,64,64]{2,1,0:T(8,128)S(1)} %reshape.335), kind=kOutput, calls=%fused_computation.15 | convolution fusion | flops 201388032 | bytes 2097152 | tf_op jit(solution)/shard_map/ky,ayz->akz/dot_general | solution.py:52
  206.6 2.3 copy.25
  210.3 3.3 %convolution_multiply_fusion.2 = f32[2048,128]{1,0:T(8,128)} fusion(f32[2048,128]{1,0:T(8,128)} %reshape.336, f32[128,128]{1,0:T(8,128)S(1)} %mul.403), kind=kOutput, calls=%fused_computation.8 | convolution fusion | flops 402915328 | bytes 2162688 | tf_op jit(solution)/shard_map/dot_general | solution.py:58
  213.8 2.2 convolution_bitcast_fusion.1
  218.0 4.8 %convolution_bitcast_fusion.7 = f32[64,64,64]{1,2,0:T(8,128)} fusion(f32[64,64,64]{2,1,0:T(8,128)S(1)} %reshape.342), kind=kOutput, calls=%fused_computation.12 | convolution fusion | flops 201388032 | bytes 2097152 | tf_op jit(solution)/shard_map/ky,ayz->akz/dot_general | solution.py:52
  226.0 2.3 fusion.71
  229.5 3.9 %convolution_bitcast_fusion = f32[1,64,4096]{2,1,0:T(8,128)} fusion(f32[64,4096]{1,0:T(8,128)} %reshape.344, f32[64,4096]{1,0:T(8,128)S(1)} %copy-done.6, f32[4096]{0:T(1024)S(1)} %add.227), kind=kOutput, calls=%fused_computation | convolution fusion | flops 204009472 | bytes 3162112 | tf_op jit(solution)/shard_map/kx,pxq->pkq/dot_general | solution.py:46
  235.6 4.8 %convolution_bitcast_fusion.6 = f32[64,64,64]{1,2,0:T(8,128)} fusion(f32[64,64,64]{2,1,0:T(8,128)S(1)} %reshape.345), kind=kOutput, calls=%fused_computation.11 | convolution fusion | flops 201388032 | bytes 2097152 | tf_op jit(solution)/shard_map/ky,ayz->akz/dot_general | solution.py:52
  243.6 2.4 convolution_multiply_fusion
  246.0 4.5 %multiply_add_fusion = f32[1,262144]{1,0:T(1,128)} fusion(f32[1,262144]{1,0:T(1,128)S(1)} %bitcast.88, f32[1,262144]{1,0:T(1,128)} %collective-permute-done.3, f32[1,262144]{1,0:T(1,128)S(1)} %bitcast.86, f32[1,262144]{1,0:T(1,128)} %collective-permute-done.2, f32[1,262144]{1,0:T(1,128)S(1)} %bitcast.87, f32[1,262144]{1,0:T(1,128)S(1)} %broadcast_select_fusion.1), kind=kLoop, calls=%fused_computation.18 | loop fusion | flops 1310720 | bytes 7340032 | tf_op jit(solution)/shard_map/add | solution.py:100
  252.2 3.7 %all-to-all-start = ((f32[1,4,16384]{2,0,1:T(1,128)}), f32[1,4,16384]{2,0,1:T(1,128)S(1)}, u32[]{:S(2)}, u32[]{:S(2)}) async-start(f32[1,4,16384]{2,0,1:T(1,128)} %bitcast.23), calls=%async_computation | async-start | bytes 524288 | tf_op jit(solution)/shard_map/all_to_all | solution.py:105
  257.2 30.9 %all-reduce.4.cloned.1.call-done = f32[1,262144]{1,0:T(1,128)} async-done(((f32[1,262144]{1,0:T(1,128)}), f32[1,262144]{1,0:T(1,128)}) %all-reduce.4.cloned.1.call-update) | async-done | bytes 1048592
  289.7 4.6 %all-to-all-start.1 = ((f32[1,4,16384]{2,0,1:T(1,128)}), f32[1,4,16384]{2,0,1:T(1,128)S(1)}, u32[]{:S(2)}, u32[]{:S(2)}) async-start(f32[1,4,16384]{2,0,1:T(1,128)} %bitcast.24), calls=%async_computation.1 | async-start | bytes 524288 | tf_op jit(solution)/shard_map/all_to_all | solution.py:106
  294.9 7.7 %all-to-all-done.1 = f32[1,4,16384]{2,0,1:T(1,128)S(1)} async-done(((f32[1,4,16384]{2,0,1:T(1,128)}), f32[1,4,16384]{2,0,1:T(1,128)S(1)}, u32[]{:S(2)}, u32[]{:S(2)}) %all-to-all-start.1) | async-done | bytes 262176 | tf_op jit(solution)/shard_map/all_to_all | solution.py:106
  304.0 9.8 %all-reduce.1 = f32[4,4]{1,0:T(4,128)S(1)} all-reduce(f32[4,4]{1,0:T(4,128)S(1)} %convolution_multiply_fusion.3), channel_id=3, replica_groups=mesh['groups'=2,'blk'=4,'rep'=4] {'blk'}, use_global_device_ids=true, to_apply=%region_1.2.clone | all-reduce | flops 16 | bytes 128
  314.4 6.2 %psum.7 = f32[1,4]{1,0:T(1,128)} all-reduce(f32[1,4]{1,0:T(1,128)S(1)} %constant_dynamic-slice_fusion), channel_id=1, replica_groups=mesh['groups'=2,'blk'=4,'rep'=4] {'rep'}, use_global_device_ids=true, to_apply=%region_2.3 | all-reduce | flops 4 | bytes 32 | tf_op jit(solution)/shard_map/psum | solution.py:112
  (66 shorter events, 50.0 us)
Async XLA Ops:
  7.2 280.9 %all-reduce.4.cloned.1.call-start = ((), (), s32[]{:S(2)}) async-start(), calls=%async_computation.2 | async-start | bytes 2097152
  7.2 28.5 %collective-permute-start = (f32[1,262144]{1,0:T(1,128)}, f32[1,262144]{1,0:T(1,128)S(1)}, u32[]{:S(2)}, u32[]{:S(2)}) collective-permute-start(f32[1,262144]{1,0:T(1,128)} %param.2), channel_id=1, source_target_pairs={{12,0},{0,4},{4,8},{8,12},{13,1},{1,5},{5,9},{9,13},{14,2},{2,6},{... | collective-permute-start | bytes 3145736 | tf_op jit(solution)/shard_map/ppermute | solution.py:16
  36.8 46.6 %collective-permute-start.1 = (f32[1,262144]{1,0:T(1,128)S(1)}, f32[1,262144]{1,0:T(1,128)S(1)}, u32[]{:S(2)}, u32[]{:S(2)}) collective-permute-start(f32[1,262144]{1,0:T(1,128)S(1)} %broadcast_select_fusion), channel_id=1, source_target_pairs={{8,0},{12,4},{0,8},{4,12},{9,1},{13,5},{1,9},{5,13},{10,2},{14,6},... | collective-permute-start | bytes 3145736 | tf_op jit(solution)/shard_map/ppermute | solution.py:16
  84.6 28.0 %collective-permute-start.2 = (f32[1,262144]{1,0:T(1,128)S(1)}, f32[1,262144]{1,0:T(1,128)}, u32[]{:S(2)}, u32[]{:S(2)}) collective-permute-start(f32[1,262144]{1,0:T(1,128)S(1)} %broadcast_select_fusion.1), channel_id=1, source_target_pairs={{12,0},{0,4},{4,8},{8,12},{13,1},{1,5},{5,9},{9,13},{14,2},{2,6},{... | collective-permute-start | bytes 3145736 | tf_op jit(solution)/shard_map/ppermute | solution.py:16
  84.6 47.7 %collective-permute-start.3 = (f32[1,262144]{1,0:T(1,128)S(1)}, f32[1,262144]{1,0:T(1,128)}, u32[]{:S(2)}, u32[]{:S(2)}) collective-permute-start(f32[1,262144]{1,0:T(1,128)S(1)} %broadcast_select_fusion.1), channel_id=1, source_target_pairs={{4,0},{8,4},{12,8},{0,12},{5,1},{9,5},{13,9},{1,13},{6,2},{10,6},{... | collective-permute-start | bytes 3145736 | tf_op jit(solution)/shard_map/ppermute | solution.py:16
  159.2 3.5 %copy-start.4 = (f32[64,4096]{1,0:T(8,128)S(1)}, f32[64,4096]{1,0:T(8,128)}, u32[]{:S(2)}) copy-start(f32[64,4096]{1,0:T(8,128)} %add.226) | copy-start | bytes 3145732
  176.6 3.3 %copy-start.3 = (f32[262144]{0:T(1024)S(1)}, f32[262144]{0:T(1024)}, u32[]{:S(2)}) copy-start(f32[262144]{0:T(1024)} %get-tuple-element.2) | copy-start | bytes 3145732
  192.5 3.5 %copy-start.5 = (f32[64,4096]{1,0:T(8,128)S(1)}, f32[64,4096]{1,0:T(8,128)}, u32[]{:S(2)}) copy-start(f32[64,4096]{1,0:T(8,128)} %add.226) | copy-start | bytes 3145732
  210.3 3.3 %copy-start.1 = (f32[262144]{0:T(1024)S(1)}, f32[262144]{0:T(1024)}, u32[]{:S(2)}) copy-start(f32[262144]{0:T(1024)} %get-tuple-element.4) | copy-start | bytes 3145732
  226.0 3.5 %copy-start.6 = (f32[64,4096]{1,0:T(8,128)S(1)}, f32[64,4096]{1,0:T(8,128)}, u32[]{:S(2)}) copy-start(f32[64,4096]{1,0:T(8,128)} %add.226) | copy-start | bytes 3145732
  243.6 2.4 copy-start
  243.6 2.4 copy-start.2
  250.5 5.4 %copy-start.8 = (u32[32]{0:T(128)S(1)}, u32[32]{0:T(128)}, u32[]{:S(2)}) copy-start(u32[32]{0:T(128)} %constant.106) | copy-start | bytes 388
  250.5 43.8 %copy-start.7 = (u32[32]{0:T(128)S(1)}, u32[32]{0:T(128)}, u32[]{:S(2)}) copy-start(u32[32]{0:T(128)} %constant.110) | copy-start | bytes 388
  252.2 37.5 %all-to-all-start = ((f32[1,4,16384]{2,0,1:T(1,128)}), f32[1,4,16384]{2,0,1:T(1,128)S(1)}, u32[]{:S(2)}, u32[]{:S(2)}) async-start(f32[1,4,16384]{2,0,1:T(1,128)} %bitcast.23), calls=%async_computation | async-start | bytes 524288 | tf_op jit(solution)/shard_map/all_to_all | solution.py:105
  289.7 12.9 %all-to-all-start.1 = ((f32[1,4,16384]{2,0,1:T(1,128)}), f32[1,4,16384]{2,0,1:T(1,128)S(1)}, u32[]{:S(2)}, u32[]{:S(2)}) async-start(f32[1,4,16384]{2,0,1:T(1,128)} %bitcast.24), calls=%async_computation.1 | async-start | bytes 524288 | tf_op jit(solution)/shard_map/all_to_all | solution.py:106
Sparse Core Ops, SparseCore 0:
  250.7 37.3 all-reduce.3
where the time goes:
time: 331 us; the launch traced here: 328 us
  waiting for transfers between devices  149 us (45%)
  matrix products  64 us (19%)
  local copies, waits for them, and re-layouts  45.4 us (14%)
  other arithmetic  21.3 us (6%)
  starting transfers between devices  16.1 us (5%)
  blocking collectives  16 us (5%)
  between operations  15.8 us (5%)
    ppermute x4, waiting for transfers between devices, passed_along(): return lax.ppermute(block, axis, route)  110 us
    unnamed x2, waiting for transfers between devices  30.9 us
    dot_general x6, matrix products, transform(): jnp.einsum('ky,ayz->akz', cas_values, values_field.reshape(batch_size * g...  28.7 us
    dot_general x6, matrix products, transform(): jnp.einsum('kx,pxq->pkq', cas_values, values_field.reshape(batch_size, gr...  18.2 us
    dot_general x6, matrix products, transform(): jnp.dot(values_field.reshape(batch_size * grid_points * grid_points // 2,...  15.8 us
    mul x1, other arithmetic, cycle_term(): own_block[:, None, :] * visiting[None, :, :]  14.2 us
    reshape x6, local copies, waits for them, and re-layouts, transform(): values_field.reshape(batch_size * grid_points, grid_points, grid_points)  12.4 us
    transpose x6, local copies, waits for them, and re-layouts, transform(): jnp.einsum('ky,ayz->akz', cas_values, values_field.reshape(batch_size * g...  12.1 us
  transfers between devices with their start and end apart: 7, of which 6 were waited for; matrix products, arithmetic and copies ran while one was open for 3% of the time, Pallas kernels for 0%

commit v1 on v0

--- a/solution.py
+++ b/solution.py
@@ -7,6 +7,8 @@
 
 
 precise_mode = lax.Precision.HIGHEST
+solve_mode = lax.Precision.HIGH
+STEPS = 3
 screen_scale = 0.05
 
 
@@ -47,18 +49,18 @@
         "kx,pxq->pkq",
         cas_values,
         values_field.reshape(batch_size, grid_points, grid_points * grid_points),
-        precision=precise_mode,
+        precision=solve_mode,
     )
     values_field = jnp.einsum(
         "ky,ayz->akz",
         cas_values,
         values_field.reshape(batch_size * grid_points, grid_points, grid_points),
-        precision=precise_mode,
+        precision=solve_mode,
     )
     values_field = jnp.dot(
         values_field.reshape(batch_size * grid_points * grid_points // 2, 2 * grid_points),
         cas_paired,
-        precision=precise_mode,
+        precision=solve_mode,
     )
     return values_field.reshape(batch_size, grid_points, grid_points, grid_points)
 
@@ -84,20 +86,8 @@
     return orbital_block
 
 
-def local(orbitals, offsets):
-    cas_values = cas_table(NG)
-    cas_paired = jnp.kron(jnp.eye(2, dtype=jnp.float32), cas_values)
-    kernel = screened_kernel(NG)
-    cycle_size = lax.axis_size("blk")
+def finish(accumulator, orbitals):
     replica = lax.axis_index("rep")
-    start_block = offsets[replica]
-    first_visit = position_block(orbitals, (start_block + 1) % cycle_size)
-    behind = passed_along(first_visit, "blk", -1)
-    accumulator = cycle_term(orbitals, first_visit, cas_values, cas_paired, kernel)
-    ahead_block = first_visit
-    ahead_block = passed_along(ahead_block, "blk", 1)
-    accumulator = accumulator + cycle_term(orbitals, ahead_block, cas_values, cas_paired, kernel)
-    accumulator = accumulator + cycle_term(orbitals, behind, cas_values, cas_paired, kernel)
     exchanged = lax.psum_scatter(accumulator, "rep", scatter_dimension=1, tiled=True)
     quarter_cells = exchanged.shape[1]
     quarter = lax.dynamic_slice_in_dim(orbitals, replica * quarter_cells, quarter_cells, 1)
@@ -113,8 +103,50 @@
     return (exchanged, margin)
 
 
+def local_steps(orbitals, offsets):
+    cas_values = cas_table(NG)
+    cas_paired = jnp.kron(jnp.eye(2, dtype=jnp.float32), cas_values)
+    kernel = screened_kernel(NG)
+    cycle_size = lax.axis_size("blk")
+    replica = lax.axis_index("rep")
+    start_block = offsets[replica]
+    first_visit = position_block(orbitals, (start_block + 1) % cycle_size)
+    behind = passed_along(first_visit, "blk", -1)
+    accumulator = cycle_term(orbitals, first_visit, cas_values, cas_paired, kernel)
+    ahead_block = passed_along(first_visit, "blk", 1)
+    accumulator = accumulator + cycle_term(orbitals, ahead_block, cas_values, cas_paired, kernel)
+    accumulator = accumulator + cycle_term(orbitals, behind, cas_values, cas_paired, kernel)
+    return finish(accumulator, orbitals)
+
+
+def distance_counts(offsets, cycle_size):
+    met = (offsets[:, None] + jnp.arange(STEPS, dtype=jnp.int32)[None, :]) % cycle_size
+    distances = jnp.arange(cycle_size, dtype=jnp.int32)
+    return jnp.sum((met[None] == distances[:, None, None]).astype(jnp.float32), axis=(1, 2))
+
+
+def local_distances(orbitals, offsets):
+    cycle_size = lax.axis_size("blk")
+    replicas = lax.axis_size("rep")
+    counts = distance_counts(offsets, cycle_size)
+    cas_values = cas_table(NG)
+    cas_paired = jnp.kron(jnp.eye(2, dtype=jnp.float32), cas_values)
+    kernel = screened_kernel(NG)
+    route = [
+        (b * replicas + d, (b + d) % cycle_size * replicas + d)
+        for b in range(cycle_size)
+        for d in range(replicas)
+    ]
+    visiting = lax.ppermute(orbitals, ("blk", "rep"), route)
+    weight = counts[lax.axis_index("rep")]
+    accumulator = weight * cycle_term(orbitals, visiting, cas_values, cas_paired, kernel)
+    return finish(accumulator, orbitals)
+
+
 def solution(mesh):
     placed = (P(("groups", "blk"), None), P("groups"))
+    one_each = mesh.shape["blk"] == mesh.shape["rep"]
+    local = local_distances if one_each else local_steps
     return jax.shard_map(
         local,
         mesh=mesh,

time: 331 us -> 168 us (0.51)
  waiting for transfers between devices: 149 us -> 72.2 us
  matrix products: 64 us -> 16.5 us
  local copies, waits for them, and re-layouts: 45.4 us -> 20.3 us
  other arithmetic: 21.3 us -> 14.9 us
    ppermute x4 -> x1, waiting for transfers between devices: 110 us -> 0.01 us  [local_distances(): visiting = lax.ppermute(orbitals, ('blk', 'rep'), route)]
    unnamed x2, waiting for transfers between devices: 30.9 us -> 64.5 us
    dot_general x6 -> x2, matrix products: 28.7 us -> 6.37 us  [transform(): jnp.einsum('ky,ayz->akz', cas_values, values_field.reshape(batch_size * g...]
    dot_general x6 -> x2, matrix products: 18.2 us -> 5.12 us  [transform(): jnp.einsum('kx,pxq->pkq', cas_values, values_field.reshape(batch_size, gr...]
    dot_general x6 -> x2, matrix products: 15.8 us -> 3.68 us  [transform(): jnp.dot(values_field.reshape(batch_size * grid_points * grid_points // 2,...]
    transpose x6 -> x2, local copies, waits for them, and re-layouts: 12.1 us -> 3.84 us  [transform(): jnp.einsum('ky,ayz->akz', cas_values, values_field.reshape(batch_size * g...]
    reshape x6 -> x2, local copies, waits for them, and re-layouts: 12.4 us -> 4.17 us  [transform(): values_field.reshape(batch_size * grid_points, grid_points, grid_points)]
    ppermute x4 -> x1, starting transfers between devices: 7.76 us -> 1.88 us  [local_distances(): visiting = lax.ppermute(orbitals, ('blk', 'rep'), route)]
  transfers between devices with their start and end apart: 7 -> 4, of which waited for: 6 -> 2; matrix products, arithmetic and copies ran while one was open for 3% -> 5% of each run, Pallas kernels for 0% -> 0%
where the time goes in v1:
time: 168 us
  waiting for transfers between devices  72.2 us (43%)
  local copies, waits for them, and re-layouts  20.3 us (12%)
  matrix products  16.5 us (10%)
  blocking collectives  16 us (10%)
  other arithmetic  14.9 us (9%)
  between operations  14.8 us (9%)
  starting transfers between devices  12.9 us (8%)
    unnamed x2, waiting for transfers between devices  64.5 us
    mul x1, other arithmetic, cycle_term(): own_block[:, None, :] * visiting[None, :, :]  11.9 us
    unnamed x1, blocking collectives  9.81 us
    all_to_all x1, waiting for transfers between devices, finish(): lax.all_to_all(exchanged, 'blk', split_axis=1, concat_axis=0, tiled=True)  7.71 us
    dot_general x2, matrix products, transform(): jnp.einsum('ky,ayz->akz', cas_values, values_field.reshape(batch_size * g...  6.37 us
    all_to_all x1, starting transfers between devices, finish(): lax.all_to_all(quarter, 'blk', split_axis=1, concat_axis=0, tiled=True)  6.35 us
    psum x1, blocking collectives, finish(): margin = lax.psum(gram_rows, 'rep')  6.17 us
    dot_general x2, matrix products, transform(): jnp.einsum('kx,pxq->pkq', cas_values, values_field.reshape(batch_size, gr...  5.12 us
  transfers between devices with their start and end apart: 4, of which 2 were waited for; matrix products, arithmetic and copies ran while one was open for 5% of the time, Pallas kernels for 0%

profile of v1, /device:TPU:0, one launch (start us, length us, event | category | flops | bytes accessed | tf_op | source)
XLA Modules:
  0.0 167.5 jit_solution(13557007717913914522)
XLA Ops:
  7.2 1.9 %collective-permute-start = (f32[1,262144]{1,0:T(1,128)}, f32[1,262144]{1,0:T(1,128)S(1)}, u32[]{:S(2)}, u32[]{:S(2)}) collective-permute-start(f32[1,262144]{1,0:T(1,128)} %param.2), channel_id=1, source_target_pairs={{0,0},{1,5},{2,10},{3,15},{4,4},{5,9},{6,14},{7,3},{8,8},{9,13},{1... | collective-permute-start | bytes 3145736 | tf_op jit(solution)/shard_map/ppermute | solution.py:140
  9.6 0.6 add.137
  10.2 1.6 add.138
  12.0 0.6 dynamic_slice.6
  12.6 11.9 %multiply_reduce_fusion = f32[262144]{0:T(1024)S(1)} fusion(f32[1,262144]{1,0:T(1,128)} %param.2, f32[1,262144]{1,0:T(1,128)S(1)} %collective-permute-done), kind=kLoop, calls=%fused_computation.16 | loop fusion | flops 262144 | bytes 3145728 | tf_op jit(solution)/shard_map/mul | solution.py:71
  24.5 0.2 mul.181
  24.7 1.7 %convolution_bitcast_fusion.1 = f32[1,64,4096]{2,1,0:T(8,128)} fusion(f32[64,4096]{1,0:T(8,128)S(1)} %mul.181), kind=kOutput, calls=%fused_computation.1 | convolution fusion | flops 100724736 | bytes 2097152 | tf_op jit(solution)/shard_map/kx,pxq->pkq/dot_general | solution.py:48
  26.4 2.0 %reshape.222 = f32[64,64,64]{2,1,0:T(8,128)S(1)} reshape(f32[1,64,4096]{2,1,0:T(8,128)} %convolution_bitcast_fusion.1) | data formatting | bytes 2097152 | tf_op jit(solution)/shard_map/reshape | solution.py:57
  28.4 3.2 %convolution_bitcast_fusion.3 = f32[64,64,64]{1,2,0:T(8,128)} fusion(f32[64,64,64]{2,1,0:T(8,128)S(1)} %reshape.222), kind=kOutput, calls=%fused_computation.4 | convolution fusion | flops 100724736 | bytes 2097152 | tf_op jit(solution)/shard_map/ky,ayz->akz/dot_general | solution.py:54
  31.6 1.9 %copy.16 = f32[64,64,64]{2,1,0:T(8,128)S(1)} copy(f32[64,64,64]{1,2,0:T(8,128)} %convolution_bitcast_fusion.3) | data formatting | bytes 2097152 | tf_op jit(solution)/shard_map/ky,ayz->akz/transpose | solution.py:54
  33.5 1.3 reshape.223
  34.9 1.9 %fusion.53 = f32[2048,128]{1,0:T(8,128)S(1)} fusion(f32[2048,128]{1,0:T(8,128)} %reshape.223, f32[128,128]{1,0:T(8,128)S(1)} %mul.190), kind=kOutput, calls=%fused_computation.77 | convolution fusion | flops 201326592 | bytes 2162688 | tf_op jit(solution)/shard_map/dot_general | solution.py:60
  36.7 1.2 reshape.224
  37.9 3.4 %convolution_bitcast_fusion = f32[1,64,4096]{2,1,0:T(8,128)} fusion(f32[64,4096]{1,0:T(8,128)} %reshape.224, f32[64,4096]{1,0:T(8,128)S(1)} %copy-done, f32[4096]{0:T(1024)S(1)} %add.139), kind=kOutput, calls=%fused_computation | convolution fusion | flops 103346176 | bytes 3162112 | tf_op jit(solution)/shard_map/kx,pxq->pkq/dot_general | solution.py:48
  41.3 2.2 %reshape.225 = f32[64,64,64]{2,1,0:T(8,128)S(1)} reshape(f32[1,64,4096]{2,1,0:T(8,128)} %convolution_bitcast_fusion) | data formatting | bytes 2097152 | tf_op jit(solution)/shard_map/reshape | solution.py:57
  43.5 3.2 %convolution_bitcast_fusion.2 = f32[64,64,64]{1,2,0:T(8,128)} fusion(f32[64,64,64]{2,1,0:T(8,128)S(1)} %reshape.225), kind=kOutput, calls=%fused_computation.3 | convolution fusion | flops 100724736 | bytes 2097152 | tf_op jit(solution)/shard_map/ky,ayz->akz/dot_general | solution.py:54
  46.7 1.9 %copy.18 = f32[64,64,64]{2,1,0:T(8,128)S(1)} copy(f32[64,64,64]{1,2,0:T(8,128)} %convolution_bitcast_fusion.2) | data formatting | bytes 2097152 | tf_op jit(solution)/shard_map/ky,ayz->akz/transpose | solution.py:54
  48.6 1.3 reshape.226
  50.0 1.8 %convolution_multiply_fusion = f32[2048,128]{1,0:T(8,128)S(1)} fusion(f32[2048,128]{1,0:T(8,128)} %reshape.226, f32[128,128]{1,0:T(8,128)S(1)} %mul.190), kind=kOutput, calls=%fused_computation.2 | convolution fusion | flops 201588736 | bytes 2162688 | tf_op jit(solution)/shard_map/dot_general | solution.py:60
  51.8 2.6 %multiply_multiply_fusion = f32[1,262144]{1,0:T(1,128)} fusion(f32[1,262144]{1,0:T(1,128)S(1)} %bitcast.38, f32[1,262144]{1,0:T(1,128)S(1)} %collective-permute-done, f32[]{:T(128)} %bitcast), kind=kLoop, calls=%fused_computation.6 | loop fusion | flops 524288 | bytes 3145732 | tf_op jit(solution)/shard_map/mul | solution.py:142
  54.4 1.7 %constant_dynamic-slice_fusion.2 = f32[1,65536]{1,0:T(1,128)} fusion(f32[1,262144]{1,0:T(1,128)} %param.2, s32[]{:T(128)S(6)} %select_n.65), kind=kLoop, calls=%fused_computation.59 | loop fusion | bytes 524292 | tf_op jit(solution)/shard_map/dynamic_slice | solution.py:93
  56.1 6.3 %all-to-all-start = ((f32[1,4,16384]{2,0,1:T(1,128)}), f32[1,4,16384]{2,0,1:T(1,128)S(1)}, u32[]{:S(2)}, u32[]{:S(2)}) async-start(f32[1,4,16384]{2,0,1:T(1,128)} %bitcast.9), calls=%async_computation | async-start | bytes 524288 | tf_op jit(solution)/shard_map/all_to_all | solution.py:95
  62.5 0.6 dynamic-slice
  63.7 64.5 %all-reduce.4.cloned.1.call-done = f32[1,262144]{1,0:T(1,128)} async-done(((f32[1,262144]{1,0:T(1,128)}), f32[1,262144]{1,0:T(1,128)}) %all-reduce.4.cloned.1.call-update) | async-done | bytes 1048592
  128.2 1.7 constant_dynamic-slice_fusion.1
  129.8 4.6 %all-to-all-start.1 = ((f32[1,4,16384]{2,0,1:T(1,128)}), f32[1,4,16384]{2,0,1:T(1,128)S(1)}, u32[]{:S(2)}, u32[]{:S(2)}) async-start(f32[1,4,16384]{2,0,1:T(1,128)} %bitcast.10), calls=%async_computation.1 | async-start | bytes 524288 | tf_op jit(solution)/shard_map/all_to_all | solution.py:96
  134.4 0.6 dynamic-slice.2
  135.0 7.7 %all-to-all-done.1 = f32[1,4,16384]{2,0,1:T(1,128)S(1)} async-done(((f32[1,4,16384]{2,0,1:T(1,128)}), f32[1,4,16384]{2,0,1:T(1,128)S(1)}, u32[]{:S(2)}, u32[]{:S(2)}) %all-to-all-start.1) | async-done | bytes 262176 | tf_op jit(solution)/shard_map/all_to_all | solution.py:96
  142.7 1.3 convolution_multiply_fusion.1
  144.0 9.8 %all-reduce.1 = f32[4,4]{1,0:T(4,128)S(1)} all-reduce(f32[4,4]{1,0:T(4,128)S(1)} %convolution_multiply_fusion.1), channel_id=3, replica_groups=mesh['groups'=2,'blk'=4,'rep'=4] {'blk'}, use_global_device_ids=true, to_apply=%region_2.3.clone | all-reduce | flops 16 | bytes 128
  153.9 0.6 constant_dynamic-slice_fusion
  154.5 6.2 %psum.7 = f32[1,4]{1,0:T(1,128)} all-reduce(f32[1,4]{1,0:T(1,128)S(1)} %constant_dynamic-slice_fusion), channel_id=1, replica_groups=mesh['groups'=2,'blk'=4,'rep'=4] {'rep'}, use_global_device_ids=true, to_apply=%region_3.4 | all-reduce | flops 4 | bytes 32 | tf_op jit(solution)/shard_map/psum | solution.py:102
  (22 shorter events, 0.8 us)
Async XLA Ops:
  7.2 121.0 %all-reduce.4.cloned.1.call-start = ((), (), s32[]{:S(2)}) async-start(), calls=%async_computation.2 | async-start | bytes 2097152
  7.2 5.4 %collective-permute-start = (f32[1,262144]{1,0:T(1,128)}, f32[1,262144]{1,0:T(1,128)S(1)}, u32[]{:S(2)}, u32[]{:S(2)}) collective-permute-start(f32[1,262144]{1,0:T(1,128)} %param.2), channel_id=1, source_target_pairs={{0,0},{1,5},{2,10},{3,15},{4,4},{5,9},{6,14},{7,3},{8,8},{9,13},{1... | collective-permute-start | bytes 3145736 | tf_op jit(solution)/shard_map/ppermute | solution.py:140
  10.2 1.7 %copy-start.1 = (s32[4]{0:T(128)S(1)}, s32[4]{0:T(128)}, u32[]{:S(2)}) copy-start(s32[4]{0:T(128)} %param.3) | copy-start | bytes 52
  34.9 3.1 %copy-start = (f32[64,4096]{1,0:T(8,128)S(1)}, f32[64,4096]{1,0:T(8,128)}, u32[]{:S(2)}) copy-start(f32[64,4096]{1,0:T(8,128)} %add.138) | copy-start | bytes 3145732
  51.8 10.7 %copy-start.3 = (u32[32]{0:T(128)S(1)}, u32[32]{0:T(128)}, u32[]{:S(2)}) copy-start(u32[32]{0:T(128)} %constant.69) | copy-start | bytes 388
  54.4 80.1 %copy-start.2 = (u32[32]{0:T(128)S(1)}, u32[32]{0:T(128)}, u32[]{:S(2)}) copy-start(u32[32]{0:T(128)} %constant.73) | copy-start | bytes 388
  56.1 73.7 %all-to-all-start = ((f32[1,4,16384]{2,0,1:T(1,128)}), f32[1,4,16384]{2,0,1:T(1,128)S(1)}, u32[]{:S(2)}, u32[]{:S(2)}) async-start(f32[1,4,16384]{2,0,1:T(1,128)} %bitcast.9), calls=%async_computation | async-start | bytes 524288 | tf_op jit(solution)/shard_map/all_to_all | solution.py:95
  129.8 12.9 %all-to-all-start.1 = ((f32[1,4,16384]{2,0,1:T(1,128)}), f32[1,4,16384]{2,0,1:T(1,128)S(1)}, u32[]{:S(2)}, u32[]{:S(2)}) async-start(f32[1,4,16384]{2,0,1:T(1,128)} %bitcast.10), calls=%async_computation.1 | async-start | bytes 524288 | tf_op jit(solution)/shard_map/all_to_all | solution.py:96
Sparse Core Ops, SparseCore 0:
  54.5 73.5 all-reduce.3

commit v2 on v1

--- a/solution.py
+++ b/solution.py
@@ -1,6 +1,11 @@
+import functools
+
 import jax
 import jax.numpy as jnp
+import numpy as np
 from jax import lax
+from jax.experimental import pallas as pl
+from jax.experimental.pallas import tpu as pltpu
 from jax.sharding import PartitionSpec as P
 
 NG = 64
@@ -119,28 +124,406 @@
     return finish(accumulator, orbitals)
 
 
-def distance_counts(offsets, cycle_size):
-    met = (offsets[:, None] + jnp.arange(STEPS, dtype=jnp.int32)[None, :]) % cycle_size
-    distances = jnp.arange(cycle_size, dtype=jnp.int32)
-    return jnp.sum((met[None] == distances[:, None, None]).astype(jnp.float32), axis=(1, 2))
+MESH = pl.DeviceIdType.MESH
+LANES = 128
+
+
+def two_halves(table):
+    high = table.astype(jnp.bfloat16)
+    low = (table - high.astype(np.float64)).astype(jnp.bfloat16)
+    return high, low
+
+
+def cas_tables(grid_points):
+    index = np.arange(grid_points)
+    angle = 2.0 * np.pi / grid_points * (np.outer(index, index) % grid_points)
+    cas = np.cos(angle) + np.sin(angle)
+    high, low = two_halves(np.kron(np.eye(2), cas))
+    last_main = np.concatenate([high, high], axis=0)
+    blocks = [cas[k::2, y::2] for k in range(2) for y in range(2)]
+    y_high, y_low = two_halves(np.concatenate(blocks, axis=0))
+    middle = np.concatenate([y_high, y_high, y_low], axis=1)
+    x_high, x_low = two_halves(cas)
+    first = np.concatenate([x_high, x_high, x_low], axis=1)
+    return [jnp.asarray(t) for t in (last_main, low, middle, first)]
+
+
+def split(values):
+    high = values.astype(jnp.bfloat16)
+    return high, (values - high.astype(jnp.float32)).astype(jnp.bfloat16)
+
+
+def dot(a, b):
+    return jnp.dot(a, b, preferred_element_type=jnp.float32)
+
+
+def last_axis(values, main_ref, low_ref):
+    high, low = split(values)
+    return dot(jnp.concatenate([high, low], axis=1), main_ref[...]) + dot(high, low_ref[...])
+
+
+def middle_axis(pair, middle_ref):
+    half = pair.shape[0]
+    high, low = split(pair)
+    terms = dot(middle_ref[...], jnp.concatenate([high, low, high], axis=0))
+    lane = lax.broadcasted_iota(jnp.int32, (half, pair.shape[1]), 1) % LANES
+    first = lane < LANES // 2
+    t = [terms[i * half : (i + 1) * half] for i in range(4)]
+    straight = jnp.where(first, t[0], t[3])
+    crossed = jnp.where(first, t[2], t[1])
+    return [
+        straight[:, at : at + LANES] + pltpu.roll(crossed[:, at : at + LANES], LANES // 2, 1)
+        for at in (0, LANES)
+    ]
+
+
+def first_axis(values, first_ref):
+    high, low = split(values)
+    return dot(first_ref[...], jnp.concatenate([high, low, high], axis=0))
+
+
+def exchange_kernel(
+    n,
+    pieces,
+    group,
+    offsets_ref,
+    psi_ref,
+    main_ref,
+    low_ref,
+    middle_ref,
+    first_ref,
+    exchanged_ref,
+    margin_ref,
+    parts,
+    met,
+    field,
+    table,
+    outgoing,
+    incoming,
+    my_rows,
+    all_rows,
+    part_sent,
+    part_got,
+    met_sent,
+    met_got,
+    local_sem,
+    term_sent,
+    term_got,
+    rows_sent,
+    rows_got,
+):
+    b = lax.axis_index("blk")
+    r = lax.axis_index("rep")
+    rows = psi_ref.shape[0]
+    quarter = rows // n
+    piece = quarter // pieces
+    plane = NG * NG // LANES
+    me = b * n + r
+
+    def device(at):
+        return {"blk": at // n, "rep": at % n}
+
+    barrier = pltpu.get_barrier_semaphore()
+    for j in range(1, n * n):
+        pl.semaphore_signal(
+            barrier, inc=1, device_id=device((me + j) % (n * n)), device_id_type=MESH
+        )
+    pl.semaphore_wait(barrier, n * n - 1)
+
+    def part_copy(c, p, to):
+        start = pl.multiple_of(r * quarter + p * piece, 8)
+        return pltpu.make_async_remote_copy(
+            src_ref=psi_ref.at[pl.ds(start, piece)],
+            dst_ref=parts.at[c, pl.ds(p * piece, piece)],
+            send_sem=part_sent.at[to, p],
+            recv_sem=part_got.at[c, p],
+            device_id={"blk": to, "rep": r},
+            device_id_type=MESH,
+        )
+
+    for p in range(pieces):
+        for j in range(1, n):
+            part_copy(b, p, (b + j) % n).start()
+
+    own_copy = pltpu.make_async_copy(psi_ref, met, local_sem.at[0])
+
+    @pl.when(r == 0)
+    def _():
+        own_copy.start()
+
+    def folded(index):
+        return jnp.where(index <= NG // 2, index, index - NG).astype(jnp.float32)
+
+    lane = lax.broadcasted_iota(jnp.int32, (NG, LANES), 1)
+    kx = folded(lax.broadcasted_iota(jnp.int32, (NG, LANES), 0))
+    kz = folded(lane % NG)
+    base = kx * kx + kz * kz
+
+    def fill(k, _):
+        ky = folded(2 * k + lane // NG)
+        k_squared = base + ky * ky
+        safe = jnp.maximum(k_squared, 1.0)
+        scaled = screen_scale * safe / (4.0 * jnp.pi)
+        screened = (1.0 - jnp.exp(-scaled)) / scaled
+        start = pl.multiple_of(k * NG, NG)
+        table[pl.ds(start, NG), :] = jnp.where(k_squared > 0.5, screened, 1.0)
+        return 0
+
+    lax.fori_loop(0, plane, fill, 0)
+
+    def met_copy(c, p, slot, d):
+        return pltpu.make_async_remote_copy(
+            src_ref=parts.at[c, pl.ds(p * piece, piece)],
+            dst_ref=met.at[pl.ds(pl.multiple_of(slot * quarter + p * piece, 8), piece)],
+            send_sem=met_sent.at[d, p],
+            recv_sem=met_got.at[slot, p],
+            device_id={"blk": b, "rep": d},
+            device_id_type=MESH,
+        )
+
+    def met_local(c, p):
+        return pltpu.make_async_copy(
+            parts.at[c, pl.ds(p * piece, piece)],
+            met.at[pl.ds(pl.multiple_of(r * quarter + p * piece, 8), piece)],
+            local_sem.at[1 + p],
+        )
+
+    order = sorted(range(1, n), key=lambda j: min(j, n - j))
+    for p in range(pieces):
+        for j in order:
+            c = (b + j) % n
+            d = (n - j) % n
+            part_copy(c, p, c).wait_recv()
+
+            @pl.when(d == r)
+            def _():
+                met_local(c, p).start()
+
+            @pl.when(d != r)
+            def _():
+                met_copy(c, p, r, d).start()
+
+    count = jnp.float32(0.0)
+    for other in range(n):
+        for step in range(STEPS):
+            count = count + jnp.where((offsets_ref[other] + step) % n == r, 1.0, 0.0)
+    scale = count / float(NG**3)
+
+    batch = 4
+
+    def forward(start):
+        density = psi_ref[pl.ds(start, batch * plane), :] * met[pl.ds(start, batch * plane), :]
+        along_z = last_axis(density, main_ref, low_ref)
+        for i in range(0, batch, 2):
+            pair = jnp.concatenate(
+                [
+                    along_z[i * plane : (i + 1) * plane],
+                    along_z[(i + 1) * plane : (i + 2) * plane],
+                ],
+                axis=1,
+            )
+            for k, out in enumerate(middle_axis(pair, middle_ref)):
+                at = pl.multiple_of(start + (i + k) * plane, plane)
+                field[pl.ds(at, plane), :] = out
+
+    @pl.when(r == 0)
+    def _():
+        own_copy.wait()
+
+    steps = piece // (batch * plane)
+    for j in range(n):
+        slot = (r + j) % n
+        for p in range(pieces):
+            if j == 0:
+
+                @pl.when(r != 0)
+                def _():
+                    met_local(b, p).wait()
+
+            else:
+
+                @pl.when(r != 0)
+                def _():
+                    met_copy(b, p, slot, slot).wait_recv()
+
+            def forward_step(i, _):
+                start = slot * quarter + p * piece + i * (batch * plane)
+                forward(pl.multiple_of(start, batch * plane))
+                return 0
+
+            lax.fori_loop(0, steps, forward_step, 0)
+
+    def across(i, _):
+        k = 2 * i
+        both = jnp.concatenate(
+            [
+                field[pl.ds(k, NG, stride=plane), :],
+                field[pl.ds(k + 1, NG, stride=plane), :],
+            ],
+            axis=1,
+        )
+        at = pl.multiple_of(k * NG, NG)
+        factor = jnp.concatenate(
+            [table[pl.ds(at, NG), :], table[pl.ds(at + NG, NG), :]], axis=1
+        )
+        back = first_axis(first_axis(both, first_ref) * factor, first_ref)
+        field[pl.ds(k, NG, stride=plane), :] = back[:, :LANES]
+        field[pl.ds(k + 1, NG, stride=plane), :] = back[:, LANES:]
+        return 0
+
+    lax.fori_loop(0, plane // 2, across, 0)
+
+    def backward(slot, i):
+        start = pl.multiple_of(slot * quarter + i * (batch * plane), batch * plane)
+        values = field[pl.ds(start, batch * plane), :]
+        turned = []
+        for k in range(0, batch, 2):
+            pair = jnp.concatenate(
+                [
+                    values[k * plane : (k + 1) * plane],
+                    values[(k + 1) * plane : (k + 2) * plane],
+                ],
+                axis=1,
+            )
+            turned += middle_axis(pair, middle_ref)
+        potential = last_axis(jnp.concatenate(turned, axis=0), main_ref, low_ref)
+        return potential * (met[pl.ds(start, batch * plane), :] * scale)
+
+    def term_copy(at, to, source):
+        return pltpu.make_async_remote_copy(
+            src_ref=outgoing.at[at],
+            dst_ref=incoming.at[source],
+            send_sem=term_sent.at[at],
+            recv_sem=term_got.at[source],
+            device_id={"blk": b, "rep": to},
+            device_id_type=MESH,
+        )
+
+    away = list(range(n - 1, 0, -1))
+    for at, j in enumerate(away):
+        slot = (r + j) % n
+
+        def send_step(i, _):
+            here = pl.multiple_of(i * (batch * plane), batch * plane)
+            outgoing[at, pl.ds(here, batch * plane), :] = backward(slot, i)
+            return 0
+
+        lax.fori_loop(0, quarter // (batch * plane), send_step, 0)
+        term_copy(at, slot, r).start()
+
+    def own_step(i, _):
+        here = pl.multiple_of(i * (batch * plane), batch * plane)
+        exchanged_ref[pl.ds(here, batch * plane), :] = backward(r, i)
+        return 0
+
+    lax.fori_loop(0, quarter // (batch * plane), own_step, 0)
+    for at, j in enumerate(away):
+        source = (r + n - j) % n
+        term_copy(at, source, source).wait_recv()
+
+    def total_step(i, sums):
+        here = pl.multiple_of(i * 64, 64)
+        total = exchanged_ref[pl.ds(here, 64), :]
+        for j in range(1, n):
+            total = total + incoming[(r + j) % n, pl.ds(here, 64), :]
+        exchanged_ref[pl.ds(here, 64), :] = total
+        mine = psi_ref[pl.ds(pl.multiple_of(r * quarter + i * 64, 64), 64), :]
+        found = [jnp.sum((mine * total).reshape(8, 8, LANES), axis=0)]
+        for j in range(1, n):
+            seen = parts[(b + j) % n, pl.ds(here, 64), :]
+            found.append(jnp.sum((seen * total).reshape(8, 8, LANES), axis=0))
+        return tuple(s + f for s, f in zip(sums, found))
+
+    zeros = jnp.zeros((8, LANES), jnp.float32)
+    sums = lax.fori_loop(0, quarter // 64, total_step, (zeros,) * n)
+    sublane = lax.broadcasted_iota(jnp.int32, (8, LANES), 0)
+    packed = jnp.zeros((8, LANES), jnp.float32)
+    for j in range(n):
+        line = jnp.sum(sums[j], axis=0, keepdims=True)
+        packed = packed + jnp.where(sublane == (b + j) % n, line, 0.0)
+    my_rows[...] = packed
+
+    def rows_copy(to, source, j):
+        return pltpu.make_async_remote_copy(
+            src_ref=my_rows,
+            dst_ref=all_rows.at[source],
+            send_sem=rows_sent.at[j],
+            recv_sem=rows_got.at[source],
+            device_id=device(to),
+            device_id_type=MESH,
+        )
+
+    for j in range(1, n * n):
+        rows_copy((me + j) % (n * n), me, j).start()
+    all_rows[me] = packed
+    for j in range(1, n * n):
+        source = (me + j) % (n * n)
+        rows_copy(source, source, j).wait_recv()
+
+    wanted = sublane == b
+    place = lax.broadcasted_iota(jnp.int32, (1, n), 1)
+    answer = jnp.zeros((1, n), jnp.float32)
+    for c in range(n):
+        whole = all_rows[c * n]
+        for k in range(1, n):
+            whole = whole + all_rows[c * n + k]
+        value = jnp.sum(jnp.where(wanted, whole, 0.0)) / float(NG**3)
+        answer = jnp.where(place == c, value, answer)
+    margin_ref[...] = answer
+
+    for j in range(1, n * n):
+        rows_copy((me + j) % (n * n), me, j).wait_send()
+    for at, j in enumerate(away):
+        term_copy(at, (r + j) % n, r).wait_send()
+    for p in range(pieces):
+        for j in range(1, n):
+            part_copy(b, p, (b + j) % n).wait_send()
+            c = (b + j) % n
+            d = (n - j) % n
+
+            @pl.when(d != r)
+            def _():
+                met_copy(c, p, r, d).wait_send()
 
 
 def local_distances(orbitals, offsets):
-    cycle_size = lax.axis_size("blk")
-    replicas = lax.axis_size("rep")
-    counts = distance_counts(offsets, cycle_size)
-    cas_values = cas_table(NG)
-    cas_paired = jnp.kron(jnp.eye(2, dtype=jnp.float32), cas_values)
-    kernel = screened_kernel(NG)
-    route = [
-        (b * replicas + d, (b + d) % cycle_size * replicas + d)
-        for b in range(cycle_size)
-        for d in range(replicas)
-    ]
-    visiting = lax.ppermute(orbitals, ("blk", "rep"), route)
-    weight = counts[lax.axis_index("rep")]
-    accumulator = weight * cycle_term(orbitals, visiting, cas_values, cas_paired, kernel)
-    return finish(accumulator, orbitals)
+    n = lax.axis_size("blk")
+    pieces = 2
+    rows = orbitals.shape[1] // LANES
+    quarter = rows // n
+    tables = cas_tables(NG)
+    f32 = jnp.float32
+    vmem = pl.BlockSpec(memory_space=pltpu.VMEM)
+    exchanged, margin = pl.pallas_call(
+        functools.partial(exchange_kernel, n, pieces, None),
+        out_shape=(
+            jax.ShapeDtypeStruct((quarter, LANES), f32),
+            jax.ShapeDtypeStruct((1, n), f32),
+        ),
+        in_specs=[pl.BlockSpec(memory_space=pltpu.SMEM)] + [vmem] * 5,
+        out_specs=(vmem, vmem),
+        scratch_shapes=[
+            pltpu.VMEM((n, quarter, LANES), f32),
+            pltpu.VMEM((rows, LANES), f32),
+            pltpu.VMEM((rows, LANES), f32),
+            pltpu.VMEM((rows, LANES), f32),
+            pltpu.VMEM((n - 1, quarter, LANES), f32),
+            pltpu.VMEM((n, quarter, LANES), f32),
+            pltpu.VMEM((8, LANES), f32),
+            pltpu.VMEM((n * n, 8, LANES), f32),
+            pltpu.SemaphoreType.DMA((n, pieces)),
+            pltpu.SemaphoreType.DMA((n, pieces)),
+            pltpu.SemaphoreType.DMA((n, pieces)),
+            pltpu.SemaphoreType.DMA((n, pieces)),
+            pltpu.SemaphoreType.DMA((1 + pieces,)),
+            pltpu.SemaphoreType.DMA((n,)),
+            pltpu.SemaphoreType.DMA((n,)),
+            pltpu.SemaphoreType.DMA((n * n,)),
+            pltpu.SemaphoreType.DMA((n * n,)),
+        ],
+        compiler_params=pltpu.CompilerParams(collective_id=0, has_side_effects=True),
+    )(offsets, orbitals.reshape(rows, LANES), *tables)
+    return exchanged.reshape(1, quarter * LANES), margin
 
 
 def solution(mesh):

time: 168 us -> 70 us (0.42)
  waiting for transfers between devices: 72.2 us -> 0 us
  Pallas kernels: 0 us -> 67 us
  local copies, waits for them, and re-layouts: 20.3 us -> 2.18 us
  matrix products: 16.5 us -> 0 us
  blocking collectives: 16 us -> 0 us
  other arithmetic: 14.9 us -> 0 us
  between operations: 14.8 us -> 0.65 us
  starting transfers between devices: 12.9 us -> 0 us
    pallas_call x0 -> x1, Pallas kernels: none -> 67 us  [local_distances(): pl.pallas_call(functools.partial(exchange_kernel, n, pieces, None), out_s...]
    unnamed x2 -> x0, waiting for transfers between devices: 64.5 us -> none
    dot_general x7 -> x0, matrix products: 16.5 us -> none  [the longest x2 6.37 us: transform(): jnp.einsum('ky,ayz->akz', cas_values, values_field.reshape(batch_size * g...]
    mul x4 -> x0, other arithmetic: 14.6 us -> none  [the longest x1 11.9 us: cycle_term(): own_block[:, None, :] * visiting[None, :, :]]
    all_to_all x2 -> x0, starting transfers between devices: 10.9 us -> none  [the longest x1 6.35 us: finish(): lax.all_to_all(quarter, 'blk', split_axis=1, concat_axis=0, tiled=True)]
    unnamed x1 -> x0, blocking collectives: 9.81 us -> none
    reshape x5 -> x0, local copies, waits for them, and re-layouts: 8.03 us -> none  [the longest x2 4.17 us: transform(): values_field.reshape(batch_size * grid_points, grid_points, grid_points)]
    all_to_all x2 -> x0, waiting for transfers between devices: 7.71 us -> none  [the longest x1 7.71 us: finish(): lax.all_to_all(exchanged, 'blk', split_axis=1, concat_axis=0, tiled=True)]
  transfers between devices with their start and end apart: 4 -> 0, of which waited for: 2 -> 0; matrix products, arithmetic and copies ran while one was open for 5% -> 0% of each run, Pallas kernels for 0% -> 0%
where the time goes in v2:
time: 70 us; the launch traced here: 69.9 us
  Pallas kernels  67 us (96%)
  local copies, waits for them, and re-layouts  2.18 us (3%)
    pallas_call x1, Pallas kernels, local_distances(): pl.pallas_call(functools.partial(exchange_kernel, n, pieces, None), out_s...  67 us
    unnamed x4, local copies, waits for them, and re-layouts  2.18 us

profile of v2, /device:TPU:0, one launch (start us, length us, event | category | flops | bytes accessed | tf_op | source)
XLA Modules:
  0.0 69.9 jit_solution(10793942568097771984)
XLA Ops:
  0.6 67.0 %shard_map.77 = (f32[512,128]{1,0:T(8,128)}, f32[1,4]{1,0:T(1,128)}) custom-call(s32[4]{0:T(128)} %offsets_ref.1, f32[2048,128]{1,0:T(8,128)} %bitcast.2, bf16[256,128]{1,0:T(8,128)(2,1)} %constant.8.clone.main_ref, bf16[128,128]{1,0:T(8,128)(2,1)} %constant.9.clone.low_ref, bf16[128,96]{1,0:T(8,128)(2,1)} %constant.10.clone.middle_ref, ...), custom_call_target="tpu_custom_call" | custom-call | tf_op jit(solution)/shard_map/pallas_call | solution.py:497
  67.7 0.0 copy-start
  67.7 1.7 %copy.10 = f32[1,65536]{1,0:T(1,128)} copy(f32[1,65536]{1,0:T(1,128)} %bitcast.3) | data formatting | bytes 524288
  69.4 0.0 copy-done
  69.4 0.5 copy.11
Async XLA Ops:
  67.7 1.7 %copy-start = (f32[1,4]{1,0:T(1,128)S(1)}, f32[1,4]{1,0:T(1,128)}, u32[]{:S(2)}) copy-start(f32[1,4]{1,0:T(1,128)} %get-tuple-element.9) | copy-start | bytes 52

commit v3 on v2

--- a/solution.py
+++ b/solution.py
@@ -185,7 +185,6 @@
 def exchange_kernel(
     n,
     pieces,
-    group,
     offsets_ref,
     psi_ref,
     main_ref,
@@ -198,17 +197,22 @@
     met,
     field,
     table,
-    outgoing,
-    incoming,
+    pair_out,
+    pair_in,
+    cross_out,
+    cross_in,
     my_rows,
     all_rows,
-    part_sent,
+    up_sent,
+    down_sent,
     part_got,
     met_sent,
     met_got,
     local_sem,
-    term_sent,
-    term_got,
+    pair_sent,
+    pair_got,
+    cross_sent,
+    cross_got,
     rows_sent,
     rows_got,
 ):
@@ -218,7 +222,12 @@
     quarter = rows // n
     piece = quarter // pieces
     plane = NG * NG // LANES
+    batch = piece // plane
     me = b * n + r
+    chips = n // 2
+    chip = r // 2
+    side = r % 2
+    partner = r + 1 - 2 * side
 
     def device(at):
         return {"blk": at // n, "rep": at % n}
@@ -230,26 +239,43 @@
         )
     pl.semaphore_wait(barrier, n * n - 1)
 
-    def part_copy(c, p, to):
-        start = pl.multiple_of(r * quarter + p * piece, 8)
+    def at_piece(p):
+        return pl.ds(pl.multiple_of(p * piece, 8), piece)
+
+    def quarter_piece(slot, p):
+        return pl.ds(pl.multiple_of(slot * quarter + p * piece, 8), piece)
+
+    def part_copy(source, c, p, to, sent):
         return pltpu.make_async_remote_copy(
-            src_ref=psi_ref.at[pl.ds(start, piece)],
-            dst_ref=parts.at[c, pl.ds(p * piece, piece)],
-            send_sem=part_sent.at[to, p],
+            src_ref=source,
+            dst_ref=parts.at[c, at_piece(p)],
+            send_sem=sent.at[c, p],
             recv_sem=part_got.at[c, p],
             device_id={"blk": to, "rep": r},
             device_id_type=MESH,
         )
 
-    for p in range(pieces):
-        for j in range(1, n):
-            part_copy(b, p, (b + j) % n).start()
-
-    own_copy = pltpu.make_async_copy(psi_ref, met, local_sem.at[0])
+    def own_copy(p, to, sent):
+        return part_copy(psi_ref.at[quarter_piece(r, p)], b, p, to, sent)
+
+    def relay_copy(c, p, to, sent):
+        return part_copy(parts.at[c, at_piece(p)], c, p, to, sent)
+
+    @pl.when(b < n - 1)
+    def _():
+        for p in range(pieces):
+            own_copy(p, b + 1, up_sent).start()
+
+    @pl.when(b > 0)
+    def _():
+        for p in range(pieces):
+            own_copy(p, b - 1, down_sent).start()
+
+    whole_copy = pltpu.make_async_copy(psi_ref, met, local_sem.at[0])
 
     @pl.when(r == 0)
     def _():
-        own_copy.start()
+        whole_copy.start()
 
     def folded(index):
         return jnp.where(index <= NG // 2, index, index - NG).astype(jnp.float32)
@@ -259,7 +285,7 @@
     kz = folded(lane % NG)
     base = kx * kx + kz * kz
 
-    def fill(k, _):
+    def fill(k):
         ky = folded(2 * k + lane // NG)
         k_squared = base + ky * ky
         safe = jnp.maximum(k_squared, 1.0)
@@ -267,14 +293,11 @@
         screened = (1.0 - jnp.exp(-scaled)) / scaled
         start = pl.multiple_of(k * NG, NG)
         table[pl.ds(start, NG), :] = jnp.where(k_squared > 0.5, screened, 1.0)
-        return 0
-
-    lax.fori_loop(0, plane, fill, 0)
 
     def met_copy(c, p, slot, d):
         return pltpu.make_async_remote_copy(
-            src_ref=parts.at[c, pl.ds(p * piece, piece)],
-            dst_ref=met.at[pl.ds(pl.multiple_of(slot * quarter + p * piece, 8), piece)],
+            src_ref=parts.at[c, at_piece(p)],
+            dst_ref=met.at[quarter_piece(slot, p)],
             send_sem=met_sent.at[d, p],
             recv_sem=met_got.at[slot, p],
             device_id={"blk": b, "rep": d},
@@ -283,159 +306,191 @@
 
     def met_local(c, p):
         return pltpu.make_async_copy(
-            parts.at[c, pl.ds(p * piece, piece)],
-            met.at[pl.ds(pl.multiple_of(r * quarter + p * piece, 8), piece)],
-            local_sem.at[1 + p],
-        )
-
-    order = sorted(range(1, n), key=lambda j: min(j, n - j))
-    for p in range(pieces):
-        for j in order:
-            c = (b + j) % n
-            d = (n - j) % n
-            part_copy(c, p, c).wait_recv()
-
-            @pl.when(d == r)
-            def _():
-                met_local(c, p).start()
-
-            @pl.when(d != r)
-            def _():
-                met_copy(c, p, r, d).start()
-
-    count = jnp.float32(0.0)
+            parts.at[c, at_piece(p)], met.at[quarter_piece(r, p)], local_sem.at[1 + p]
+        )
+
+    def planes_of(values):
+        return [values[i * plane : (i + 1) * plane] for i in range(batch)]
+
+    def middle_all(values):
+        whole = planes_of(values)
+        turned = []
+        for i in range(0, batch, 2):
+            pair = jnp.concatenate([whole[i], whole[i + 1]], axis=1)
+            turned += middle_axis(pair, middle_ref)
+        return jnp.concatenate(turned, axis=0)
+
+    def forward(slot, p):
+        here = quarter_piece(slot, p)
+        density = psi_ref[here, :] * met[here, :]
+        field[here, :] = middle_all(last_axis(density, main_ref, low_ref))
+
+    def forward_met(p):
+        met_local(b, p).wait()
+        forward(r, p)
+
+        def one(j, _):
+            slot = (r + j) % n
+            met_copy(b, p, slot, slot).wait_recv()
+            forward(slot, p)
+            return 0
+
+        lax.fori_loop(1, n, one, 0)
+
+    count = (n - 1) * pieces
+    fills = pl.cdiv(plane, count)
+    wanted_block = (b - r + n) % n
+    wanted_steps = jnp.maximum(wanted_block - b, b - wanted_block)
+
+    @pl.when(r == 0)
+    def _():
+        whole_copy.wait()
+
+        def one(t, _):
+            forward(t // pieces, t % pieces)
+            return 0
+
+        lax.fori_loop(0, n * pieces, one, 0)
+
+    def arrived(c, p, to, sent):
+        relay_copy(c, p, to, sent).wait_recv()
+
+        @pl.when((to >= 0) & (to < n))
+        def _():
+            relay_copy(c, p, to, sent).start()
+
+        d = (b - c + n) % n
+
+        @pl.when(d == r)
+        def _():
+            met_local(c, p).start()
+
+        @pl.when(d != r)
+        def _():
+            met_copy(c, p, r, d).start()
+
+    def relay_step(t, _):
+        for i in range(fills):
+            fill(t * fills + i)
+        k = 1 + t // pieces
+        p = t % pieces
+
+        @pl.when(b - k >= 0)
+        def _():
+            arrived(b - k, p, b + 1, up_sent)
+
+        @pl.when(b + k < n)
+        def _():
+            arrived(b + k, p, b - 1, down_sent)
+
+        before = jnp.maximum(t - 1, 0)
+
+        @pl.when((r != 0) & (t > 0) & (1 + before // pieces == wanted_steps))
+        def _():
+            forward_met(before % pieces)
+
+        return 0
+
+    lax.fori_loop(0, count, relay_step, 0)
+
+    @pl.when((r != 0) & (wanted_steps == n - 1))
+    def _():
+        forward_met(pieces - 1)
+
+    weight = jnp.float32(0.0)
     for other in range(n):
         for step in range(STEPS):
-            count = count + jnp.where((offsets_ref[other] + step) % n == r, 1.0, 0.0)
-    scale = count / float(NG**3)
-
-    batch = 4
-
-    def forward(start):
-        density = psi_ref[pl.ds(start, batch * plane), :] * met[pl.ds(start, batch * plane), :]
-        along_z = last_axis(density, main_ref, low_ref)
-        for i in range(0, batch, 2):
-            pair = jnp.concatenate(
-                [
-                    along_z[i * plane : (i + 1) * plane],
-                    along_z[(i + 1) * plane : (i + 2) * plane],
-                ],
-                axis=1,
-            )
-            for k, out in enumerate(middle_axis(pair, middle_ref)):
-                at = pl.multiple_of(start + (i + k) * plane, plane)
-                field[pl.ds(at, plane), :] = out
-
-    @pl.when(r == 0)
-    def _():
-        own_copy.wait()
-
-    steps = piece // (batch * plane)
-    for j in range(n):
-        slot = (r + j) % n
-        for p in range(pieces):
-            if j == 0:
-
-                @pl.when(r != 0)
-                def _():
-                    met_local(b, p).wait()
-
-            else:
-
-                @pl.when(r != 0)
-                def _():
-                    met_copy(b, p, slot, slot).wait_recv()
-
-            def forward_step(i, _):
-                start = slot * quarter + p * piece + i * (batch * plane)
-                forward(pl.multiple_of(start, batch * plane))
-                return 0
-
-            lax.fori_loop(0, steps, forward_step, 0)
+            weight = weight + jnp.where((offsets_ref[other] + step) % n == r, 1.0, 0.0)
+    scale = weight / float(NG**3)
+
+    wide = 4
 
     def across(i, _):
-        k = 2 * i
+        k = wide * i
         both = jnp.concatenate(
-            [
-                field[pl.ds(k, NG, stride=plane), :],
-                field[pl.ds(k + 1, NG, stride=plane), :],
-            ],
-            axis=1,
-        )
-        at = pl.multiple_of(k * NG, NG)
+            [field[pl.ds(k + w, NG, stride=plane), :] for w in range(wide)], axis=1
+        )
         factor = jnp.concatenate(
-            [table[pl.ds(at, NG), :], table[pl.ds(at + NG, NG), :]], axis=1
+            [table[pl.ds(pl.multiple_of((k + w) * NG, NG), NG), :] for w in range(wide)], axis=1
         )
         back = first_axis(first_axis(both, first_ref) * factor, first_ref)
-        field[pl.ds(k, NG, stride=plane), :] = back[:, :LANES]
-        field[pl.ds(k + 1, NG, stride=plane), :] = back[:, LANES:]
+        for w in range(wide):
+            field[pl.ds(k + w, NG, stride=plane), :] = back[:, w * LANES : (w + 1) * LANES]
         return 0
 
-    lax.fori_loop(0, plane // 2, across, 0)
-
-    def backward(slot, i):
-        start = pl.multiple_of(slot * quarter + i * (batch * plane), batch * plane)
-        values = field[pl.ds(start, batch * plane), :]
-        turned = []
-        for k in range(0, batch, 2):
-            pair = jnp.concatenate(
-                [
-                    values[k * plane : (k + 1) * plane],
-                    values[(k + 1) * plane : (k + 2) * plane],
-                ],
-                axis=1,
-            )
-            turned += middle_axis(pair, middle_ref)
-        potential = last_axis(jnp.concatenate(turned, axis=0), main_ref, low_ref)
-        return potential * (met[pl.ds(start, batch * plane), :] * scale)
-
-    def term_copy(at, to, source):
+    lax.fori_loop(0, plane // wide, across, 0)
+
+    def backward(slot, p):
+        here = quarter_piece(slot, p)
+        potential = last_axis(middle_all(field[here, :]), main_ref, low_ref)
+        return potential * (met[here, :] * scale)
+
+    def pair_copy(i, p):
         return pltpu.make_async_remote_copy(
-            src_ref=outgoing.at[at],
-            dst_ref=incoming.at[source],
-            send_sem=term_sent.at[at],
-            recv_sem=term_got.at[source],
-            device_id={"blk": b, "rep": to},
+            src_ref=pair_out.at[i, at_piece(p)],
+            dst_ref=pair_in.at[i, at_piece(p)],
+            send_sem=pair_sent.at[i, p],
+            recv_sem=pair_got.at[i, p],
+            device_id={"blk": b, "rep": partner},
             device_id_type=MESH,
         )
 
-    away = list(range(n - 1, 0, -1))
-    for at, j in enumerate(away):
-        slot = (r + j) % n
-
-        def send_step(i, _):
-            here = pl.multiple_of(i * (batch * plane), batch * plane)
-            outgoing[at, pl.ds(here, batch * plane), :] = backward(slot, i)
+    def cross_copy(i, p):
+        return pltpu.make_async_remote_copy(
+            src_ref=cross_out.at[i, at_piece(p)],
+            dst_ref=cross_in.at[chips - i, at_piece(p)],
+            send_sem=cross_sent.at[i, p],
+            recv_sem=cross_got.at[chips - i, p],
+            device_id={"blk": b, "rep": (chip + i) % chips * 2 + side},
+            device_id_type=MESH,
+        )
+
+    def pair_quarter(i):
+        def one(p, _):
+            pair_out[i, at_piece(p), :] = backward((chip + i) % chips * 2 + 1 - side, p)
+            pair_copy(i, p).start()
             return 0
 
-        lax.fori_loop(0, quarter // (batch * plane), send_step, 0)
-        term_copy(at, slot, r).start()
-
-    def own_step(i, _):
-        here = pl.multiple_of(i * (batch * plane), batch * plane)
-        exchanged_ref[pl.ds(here, batch * plane), :] = backward(r, i)
+        lax.fori_loop(0, pieces, one, 0)
+
+    for i in range(1, chips):
+        pair_quarter(i)
+
+        def cross_step(p, _):
+            mine = backward((chip + i) % chips * 2 + side, p)
+            pair_copy(i, p).wait_recv()
+            cross_out[i, at_piece(p), :] = mine + pair_in[i, at_piece(p), :]
+            cross_copy(i, p).start()
+            return 0
+
+        lax.fori_loop(0, pieces, cross_step, 0)
+    pair_quarter(0)
+
+    def own_step(p, _):
+        exchanged_ref[at_piece(p), :] = backward(r, p)
         return 0
 
-    lax.fori_loop(0, quarter // (batch * plane), own_step, 0)
-    for at, j in enumerate(away):
-        source = (r + n - j) % n
-        term_copy(at, source, source).wait_recv()
-
-    def total_step(i, sums):
-        here = pl.multiple_of(i * 64, 64)
-        total = exchanged_ref[pl.ds(here, 64), :]
+    lax.fori_loop(0, pieces, own_step, 0)
+
+    def total_step(p, sums):
+        here = at_piece(p)
+        pair_copy(0, p).wait_recv()
+        total = exchanged_ref[here, :] + pair_in[0, here, :]
+        for i in range(1, chips):
+            cross_copy(chips - i, p).wait_recv()
+            total = total + cross_in[i, here, :]
+        exchanged_ref[here, :] = total
+
+        def folded_sum(values):
+            return jnp.sum((values * total).reshape(piece // 8, 8, LANES), axis=0)
+
+        found = [folded_sum(psi_ref[quarter_piece(r, p), :])]
         for j in range(1, n):
-            total = total + incoming[(r + j) % n, pl.ds(here, 64), :]
-        exchanged_ref[pl.ds(here, 64), :] = total
-        mine = psi_ref[pl.ds(pl.multiple_of(r * quarter + i * 64, 64), 64), :]
-        found = [jnp.sum((mine * total).reshape(8, 8, LANES), axis=0)]
-        for j in range(1, n):
-            seen = parts[(b + j) % n, pl.ds(here, 64), :]
-            found.append(jnp.sum((seen * total).reshape(8, 8, LANES), axis=0))
+            found.append(folded_sum(parts[(b + j) % n, here, :]))
         return tuple(s + f for s, f in zip(sums, found))
 
     zeros = jnp.zeros((8, LANES), jnp.float32)
-    sums = lax.fori_loop(0, quarter // 64, total_step, (zeros,) * n)
+    sums = lax.fori_loop(0, pieces, total_step, (zeros,) * n)
     sublane = lax.broadcasted_iota(jnp.int32, (8, LANES), 0)
     packed = jnp.zeros((8, LANES), jnp.float32)
     for j in range(n):
@@ -473,29 +528,67 @@
 
     for j in range(1, n * n):
         rows_copy((me + j) % (n * n), me, j).wait_send()
-    for at, j in enumerate(away):
-        term_copy(at, (r + j) % n, r).wait_send()
-    for p in range(pieces):
-        for j in range(1, n):
-            part_copy(b, p, (b + j) % n).wait_send()
-            c = (b + j) % n
-            d = (n - j) % n
-
-            @pl.when(d != r)
-            def _():
-                met_copy(c, p, r, d).wait_send()
+
+    def sent_terms(p, _):
+        for i in range(chips):
+            pair_copy(i, p).wait_send()
+        for i in range(1, chips):
+            cross_copy(i, p).wait_send()
+
+        @pl.when(b < n - 1)
+        def _():
+            own_copy(p, b + 1, up_sent).wait_send()
+
+        @pl.when(b > 0)
+        def _():
+            own_copy(p, b - 1, down_sent).wait_send()
+
+        return 0
+
+    lax.fori_loop(0, pieces, sent_terms, 0)
+
+    def left(c, p, to, sent):
+        @pl.when((to >= 0) & (to < n))
+        def _():
+            relay_copy(c, p, to, sent).wait_send()
+
+        d = (b - c + n) % n
+
+        @pl.when(d != r)
+        def _():
+            met_copy(c, p, r, d).wait_send()
+
+    def sent_step(t, _):
+        k = 1 + t // pieces
+        p = t % pieces
+
+        @pl.when(b - k >= 0)
+        def _():
+            left(b - k, p, b + 1, up_sent)
+
+        @pl.when(b + k < n)
+        def _():
+            left(b + k, p, b - 1, down_sent)
+
+        return 0
+
+    lax.fori_loop(0, count, sent_step, 0)
 
 
 def local_distances(orbitals, offsets):
     n = lax.axis_size("blk")
-    pieces = 2
+    pieces = 4
     rows = orbitals.shape[1] // LANES
     quarter = rows // n
+    chips = n // 2
+    plane = NG * NG // LANES
+    fills = pl.cdiv(plane, (n - 1) * pieces) * (n - 1) * pieces
     tables = cas_tables(NG)
     f32 = jnp.float32
     vmem = pl.BlockSpec(memory_space=pltpu.VMEM)
+    dma = pltpu.SemaphoreType.DMA
     exchanged, margin = pl.pallas_call(
-        functools.partial(exchange_kernel, n, pieces, None),
+        functools.partial(exchange_kernel, n, pieces),
         out_shape=(
             jax.ShapeDtypeStruct((quarter, LANES), f32),
             jax.ShapeDtypeStruct((1, n), f32),
@@ -506,29 +599,36 @@
             pltpu.VMEM((n, quarter, LANES), f32),
             pltpu.VMEM((rows, LANES), f32),
             pltpu.VMEM((rows, LANES), f32),
-            pltpu.VMEM((rows, LANES), f32),
-            pltpu.VMEM((n - 1, quarter, LANES), f32),
-            pltpu.VMEM((n, quarter, LANES), f32),
+            pltpu.VMEM((fills * NG, LANES), f32),
+            pltpu.VMEM((chips, quarter, LANES), f32),
+            pltpu.VMEM((chips, quarter, LANES), f32),
+            pltpu.VMEM((chips, quarter, LANES), f32),
+            pltpu.VMEM((chips, quarter, LANES), f32),
             pltpu.VMEM((8, LANES), f32),
             pltpu.VMEM((n * n, 8, LANES), f32),
-            pltpu.SemaphoreType.DMA((n, pieces)),
-            pltpu.SemaphoreType.DMA((n, pieces)),
-            pltpu.SemaphoreType.DMA((n, pieces)),
-            pltpu.SemaphoreType.DMA((n, pieces)),
-            pltpu.SemaphoreType.DMA((1 + pieces,)),
-            pltpu.SemaphoreType.DMA((n,)),
-            pltpu.SemaphoreType.DMA((n,)),
-            pltpu.SemaphoreType.DMA((n * n,)),
-            pltpu.SemaphoreType.DMA((n * n,)),
+            dma((n, pieces)),
+            dma((n, pieces)),
+            dma((n, pieces)),
+            dma((n, pieces)),
+            dma((n, pieces)),
+            dma((1 + pieces,)),
+            dma((chips, pieces)),
+            dma((chips, pieces)),
+            dma((chips, pieces)),
+            dma((chips, pieces)),
+            dma((n * n,)),
+            dma((n * n,)),
         ],
-        compiler_params=pltpu.CompilerParams(collective_id=0, has_side_effects=True),
+        compiler_params=pltpu.CompilerParams(
+            collective_id=0, has_side_effects=True, vmem_limit_bytes=16 << 20
+        ),
     )(offsets, orbitals.reshape(rows, LANES), *tables)
     return exchanged.reshape(1, quarter * LANES), margin
 
 
 def solution(mesh):
     placed = (P(("groups", "blk"), None), P("groups"))
-    one_each = mesh.shape["blk"] == mesh.shape["rep"]
+    one_each = mesh.shape["blk"] == mesh.shape["rep"] and mesh.shape["rep"] % 2 == 0
     local = local_distances if one_each else local_steps
     return jax.shard_map(
         local,

time: 70 us -> 61.6 us (0.88)
  Pallas kernels: 67 us -> 54.4 us
  local copies, waits for them, and re-layouts: 2.18 us -> 6.2 us
    pallas_call x1, Pallas kernels: 67 us -> 54.4 us  [local_distances(): pl.pallas_call(functools.partial(exchange_kernel, n, pieces), out_shape=(...]
    unnamed x4 -> x14, local copies, waits for them, and re-layouts: 2.18 us -> 6.2 us
where the time goes in v3:
time: 61.6 us; the launch traced here: 61.2 us
  Pallas kernels  54.4 us (88%)
  local copies, waits for them, and re-layouts  6.2 us (10%)
  between operations  0.65 us (1%)
    pallas_call x1, Pallas kernels, local_distances(): pl.pallas_call(functools.partial(exchange_kernel, n, pieces), out_shape=(...  54.4 us
    unnamed x14, local copies, waits for them, and re-layouts  6.2 us

profile of v3, /device:TPU:0, one launch (start us, length us, event | category | flops | bytes accessed | tf_op | source)
XLA Modules:
  0.0 61.2 jit_solution(6903327688374172646)
XLA Ops:
  0.6 0.0 copy-start.5
  0.6 0.6 %copy-done.5 = s32[4]{0:T(128)S(1)} copy-done((s32[4]{0:T(128)S(1)}, s32[4]{0:T(128)}, u32[]{:S(2)}) %copy-start.5) | copy-done | bytes 40
  1.3 0.0 copy-start
  1.3 1.2 %copy-done = f32[1,262144]{1,0:T(1,128)S(1)} copy-done((f32[1,262144]{1,0:T(1,128)S(1)}, f32[1,262144]{1,0:T(1,128)}, u32[]{:S(2)}) %copy-start) | copy-done | bytes 1048600
  2.5 0.0 copy-start.1
  2.5 0.8 %copy-done.1 = bf16[256,128]{1,0:T(8,128)(2,1)S(1)} copy-done((bf16[256,128]{1,0:T(8,128)(2,1)S(1)}, bf16[256,128]{1,0:T(8,128)(2,1)}, u32[]{:S(2)}) %copy-start.1) | copy-done | bytes 65560
  3.4 0.0 copy-start.2
  3.4 0.8 %copy-done.2 = bf16[64,192]{1,0:T(8,128)(2,1)S(1)} copy-done((bf16[64,192]{1,0:T(8,128)(2,1)S(1)}, bf16[64,192]{1,0:T(8,128)(2,1)}, u32[]{:S(2)}) %copy-start.2) | copy-done | bytes 24600
  4.1 0.0 copy-start.3
  4.1 0.8 %copy-done.3 = bf16[128,96]{1,0:T(8,128)(2,1)S(1)} copy-done((bf16[128,96]{1,0:T(8,128)(2,1)S(1)}, bf16[128,96]{1,0:T(8,128)(2,1)}, u32[]{:S(2)}) %copy-start.3) | copy-done | bytes 24600
  4.9 0.0 copy-start.4
  4.9 0.8 %copy-done.4 = bf16[128,128]{1,0:T(8,128)(2,1)S(1)} copy-done((bf16[128,128]{1,0:T(8,128)(2,1)S(1)}, bf16[128,128]{1,0:T(8,128)(2,1)}, u32[]{:S(2)}) %copy-start.4) | copy-done | bytes 32792
  5.6 54.4 %shard_map.77 = (f32[512,128]{1,0:T(8,128)S(1)}, f32[1,4]{1,0:T(1,128)S(1)}) custom-call(s32[4]{0:T(128)S(1)} %copy-done.5, f32[2048,128]{1,0:T(8,128)S(1)} %bitcast.2, bf16[256,128]{1,0:T(8,128)(2,1)S(1)} %copy-done.1, bf16[128,128]{1,0:T(8,128)(2,1)S(1)} %copy-done.4, bf16[128,96]{1,0:T(8,128)(2,1)S(1)} %copy-done.3, bf16[64,192]{1,0:T(8,128)(2,1)S(1)} %copy-done.2), custom_call_target="tpu_custom_call" | custom-call | tf_op jit(solution)/shard_map/pallas_call | solution.py:590
  60.0 0.7 %copy.10 = f32[1,65536]{1,0:T(1,128)} copy(f32[1,65536]{1,0:T(1,128)S(1)} %bitcast.3) | data formatting | bytes 524288
  60.7 0.5 copy.11
Async XLA Ops:
  0.6 0.7 %copy-start.5 = (s32[4]{0:T(128)S(1)}, s32[4]{0:T(128)}, u32[]{:S(2)}) copy-start(s32[4]{0:T(128)} %offsets_ref.1) | copy-start | bytes 52
  1.3 1.2 %copy-start = (f32[1,262144]{1,0:T(1,128)S(1)}, f32[1,262144]{1,0:T(1,128)}, u32[]{:S(2)}) copy-start(f32[1,262144]{1,0:T(1,128)} %param.6) | copy-start | bytes 3145732
  2.5 0.8 %copy-start.1 = (bf16[256,128]{1,0:T(8,128)(2,1)S(1)}, bf16[256,128]{1,0:T(8,128)(2,1)}, u32[]{:S(2)}) copy-start(bf16[256,128]{1,0:T(8,128)(2,1)} %constant.8.clone.main_ref) | copy-start | bytes 196612
  3.4 0.8 %copy-start.2 = (bf16[64,192]{1,0:T(8,128)(2,1)S(1)}, bf16[64,192]{1,0:T(8,128)(2,1)}, u32[]{:S(2)}) copy-start(bf16[64,192]{1,0:T(8,128)(2,1)} %constant.11.clone.first_ref) | copy-start | bytes 73732
  4.1 0.8 %copy-start.3 = (bf16[128,96]{1,0:T(8,128)(2,1)S(1)}, bf16[128,96]{1,0:T(8,128)(2,1)}, u32[]{:S(2)}) copy-start(bf16[128,96]{1,0:T(8,128)(2,1)} %constant.10.clone.middle_ref) | copy-start | bytes 73732
  4.9 0.8 %copy-start.4 = (bf16[128,128]{1,0:T(8,128)(2,1)S(1)}, bf16[128,128]{1,0:T(8,128)(2,1)}, u32[]{:S(2)}) copy-start(bf16[128,128]{1,0:T(8,128)(2,1)} %constant.9.clone.low_ref) | copy-start | bytes 98308

commit v4 on v3

--- a/solution.py
+++ b/solution.py
@@ -403,7 +403,7 @@
             weight = weight + jnp.where((offsets_ref[other] + step) % n == r, 1.0, 0.0)
     scale = weight / float(NG**3)
 
-    wide = 4
+    wide = 16
 
     def across(i, _):
         k = wide * i
@@ -577,7 +577,7 @@
 
 def local_distances(orbitals, offsets):
     n = lax.axis_size("blk")
-    pieces = 4
+    pieces = 2
     rows = orbitals.shape[1] // LANES
     quarter = rows // n
     chips = n // 2

time: 61.6 us -> 53.7 us (0.87)
  Pallas kernels: 54.4 us -> 46.5 us
    pallas_call x1, Pallas kernels: 54.4 us -> 46.5 us  [local_distances(): pl.pallas_call(functools.partial(exchange_kernel, n, pieces), out_shape=(...]
where the time goes in v4:
time: 53.7 us; the launch traced here: 53.3 us
  Pallas kernels  46.5 us (87%)
  local copies, waits for them, and re-layouts  6.2 us (12%)
  between operations  0.65 us (1%)
    pallas_call x1, Pallas kernels, local_distances(): pl.pallas_call(functools.partial(exchange_kernel, n, pieces), out_shape=(...  46.5 us
    unnamed x14, local copies, waits for them, and re-layouts  6.2 us

profile of v4, /device:TPU:0, one launch (start us, length us, event | category | flops | bytes accessed | tf_op | source)
XLA Modules:
  0.0 53.3 jit_solution(4972683007424055653)
XLA Ops:
  0.6 0.0 copy-start.5
  0.6 0.6 %copy-done.5 = s32[4]{0:T(128)S(1)} copy-done((s32[4]{0:T(128)S(1)}, s32[4]{0:T(128)}, u32[]{:S(2)}) %copy-start.5) | copy-done | bytes 40
  1.3 0.0 copy-start
  1.3 1.2 %copy-done = f32[1,262144]{1,0:T(1,128)S(1)} copy-done((f32[1,262144]{1,0:T(1,128)S(1)}, f32[1,262144]{1,0:T(1,128)}, u32[]{:S(2)}) %copy-start) | copy-done | bytes 1048600
  2.5 0.0 copy-start.1
  2.5 0.8 %copy-done.1 = bf16[256,128]{1,0:T(8,128)(2,1)S(1)} copy-done((bf16[256,128]{1,0:T(8,128)(2,1)S(1)}, bf16[256,128]{1,0:T(8,128)(2,1)}, u32[]{:S(2)}) %copy-start.1) | copy-done | bytes 65560
  3.4 0.0 copy-start.2
  3.4 0.8 %copy-done.2 = bf16[64,192]{1,0:T(8,128)(2,1)S(1)} copy-done((bf16[64,192]{1,0:T(8,128)(2,1)S(1)}, bf16[64,192]{1,0:T(8,128)(2,1)}, u32[]{:S(2)}) %copy-start.2) | copy-done | bytes 24600
  4.1 0.0 copy-start.3
  4.1 0.8 %copy-done.3 = bf16[128,96]{1,0:T(8,128)(2,1)S(1)} copy-done((bf16[128,96]{1,0:T(8,128)(2,1)S(1)}, bf16[128,96]{1,0:T(8,128)(2,1)}, u32[]{:S(2)}) %copy-start.3) | copy-done | bytes 24600
  4.9 0.0 copy-start.4
  4.9 0.8 %copy-done.4 = bf16[128,128]{1,0:T(8,128)(2,1)S(1)} copy-done((bf16[128,128]{1,0:T(8,128)(2,1)S(1)}, bf16[128,128]{1,0:T(8,128)(2,1)}, u32[]{:S(2)}) %copy-start.4) | copy-done | bytes 32792
  5.6 46.5 %shard_map.77 = (f32[512,128]{1,0:T(8,128)S(1)}, f32[1,4]{1,0:T(1,128)S(1)}) custom-call(s32[4]{0:T(128)S(1)} %copy-done.5, f32[2048,128]{1,0:T(8,128)S(1)} %bitcast.2, bf16[256,128]{1,0:T(8,128)(2,1)S(1)} %copy-done.1, bf16[128,128]{1,0:T(8,128)(2,1)S(1)} %copy-done.4, bf16[128,96]{1,0:T(8,128)(2,1)S(1)} %copy-done.3, bf16[64,192]{1,0:T(8,128)(2,1)S(1)} %copy-done.2), custom_call_target="tpu_custom_call" | custom-call | tf_op jit(solution)/shard_map/pallas_call | solution.py:590
  52.1 0.7 %copy.10 = f32[1,65536]{1,0:T(1,128)} copy(f32[1,65536]{1,0:T(1,128)S(1)} %bitcast.3) | data formatting | bytes 524288
  52.8 0.5 copy.11
Async XLA Ops:
  0.6 0.7 %copy-start.5 = (s32[4]{0:T(128)S(1)}, s32[4]{0:T(128)}, u32[]{:S(2)}) copy-start(s32[4]{0:T(128)} %offsets_ref.1) | copy-start | bytes 52
  1.3 1.2 %copy-start = (f32[1,262144]{1,0:T(1,128)S(1)}, f32[1,262144]{1,0:T(1,128)}, u32[]{:S(2)}) copy-start(f32[1,262144]{1,0:T(1,128)} %param.6) | copy-start | bytes 3145732
  2.5 0.8 %copy-start.1 = (bf16[256,128]{1,0:T(8,128)(2,1)S(1)}, bf16[256,128]{1,0:T(8,128)(2,1)}, u32[]{:S(2)}) copy-start(bf16[256,128]{1,0:T(8,128)(2,1)} %constant.8.clone.main_ref) | copy-start | bytes 196612
  3.4 0.8 %copy-start.2 = (bf16[64,192]{1,0:T(8,128)(2,1)S(1)}, bf16[64,192]{1,0:T(8,128)(2,1)}, u32[]{:S(2)}) copy-start(bf16[64,192]{1,0:T(8,128)(2,1)} %constant.11.clone.first_ref) | copy-start | bytes 73732
  4.1 0.8 %copy-start.3 = (bf16[128,96]{1,0:T(8,128)(2,1)S(1)}, bf16[128,96]{1,0:T(8,128)(2,1)}, u32[]{:S(2)}) copy-start(bf16[128,96]{1,0:T(8,128)(2,1)} %constant.10.clone.middle_ref) | copy-start | bytes 73732
  4.9 0.8 %copy-start.4 = (bf16[128,128]{1,0:T(8,128)(2,1)S(1)}, bf16[128,128]{1,0:T(8,128)(2,1)}, u32[]{:S(2)}) copy-start(bf16[128,128]{1,0:T(8,128)(2,1)} %constant.9.clone.low_ref) | copy-start | bytes 98308

commit v5 on v4

--- a/solution.py
+++ b/solution.py
@@ -339,18 +339,13 @@
 
     count = (n - 1) * pieces
     fills = pl.cdiv(plane, count)
+    own_batches = pl.cdiv(n * pieces, count)
     wanted_block = (b - r + n) % n
     wanted_steps = jnp.maximum(wanted_block - b, b - wanted_block)
 
     @pl.when(r == 0)
     def _():
         whole_copy.wait()
-
-        def one(t, _):
-            forward(t // pieces, t % pieces)
-            return 0
-
-        lax.fori_loop(0, n * pieces, one, 0)
 
     def arrived(c, p, to, sent):
         relay_copy(c, p, to, sent).wait_recv()
@@ -382,6 +377,19 @@
         @pl.when(b + k < n)
         def _():
             arrived(b + k, p, b - 1, down_sent)
+
+        def own_forward(i, _):
+            at = t * own_batches + i
+
+            @pl.when(at < n * pieces)
+            def _():
+                forward(at // pieces, at % pieces)
+
+            return 0
+
+        @pl.when(r == 0)
+        def _():
+            lax.fori_loop(0, own_batches, own_forward, 0)
 
         before = jnp.maximum(t - 1, 0)
 

time: 53.7 us -> 53.8 us (level)
  no operation moved by 1% of the time
where the time goes in v5:
time: 53.8 us; the launch traced here: 53.4 us
  Pallas kernels  46.5 us (86%)
  local copies, waits for them, and re-layouts  6.2 us (12%)
  between operations  0.65 us (1%)
    pallas_call x1, Pallas kernels, local_distances(): pl.pallas_call(functools.partial(exchange_kernel, n, pieces), out_shape=(...  46.5 us
    unnamed x14, local copies, waits for them, and re-layouts  6.2 us

profile of v5, /device:TPU:0, one launch (start us, length us, event | category | flops | bytes accessed | tf_op | source)
XLA Modules:
  0.0 53.4 jit_solution(17369103685246661854)
XLA Ops:
  0.6 0.0 copy-start.5
  0.6 0.6 %copy-done.5 = s32[4]{0:T(128)S(1)} copy-done((s32[4]{0:T(128)S(1)}, s32[4]{0:T(128)}, u32[]{:S(2)}) %copy-start.5) | copy-done | bytes 40
  1.3 0.0 copy-start
  1.3 1.2 %copy-done = f32[1,262144]{1,0:T(1,128)S(1)} copy-done((f32[1,262144]{1,0:T(1,128)S(1)}, f32[1,262144]{1,0:T(1,128)}, u32[]{:S(2)}) %copy-start) | copy-done | bytes 1048600
  2.5 0.0 copy-start.1
  2.5 0.8 %copy-done.1 = bf16[256,128]{1,0:T(8,128)(2,1)S(1)} copy-done((bf16[256,128]{1,0:T(8,128)(2,1)S(1)}, bf16[256,128]{1,0:T(8,128)(2,1)}, u32[]{:S(2)}) %copy-start.1) | copy-done | bytes 65560
  3.4 0.0 copy-start.2
  3.4 0.8 %copy-done.2 = bf16[64,192]{1,0:T(8,128)(2,1)S(1)} copy-done((bf16[64,192]{1,0:T(8,128)(2,1)S(1)}, bf16[64,192]{1,0:T(8,128)(2,1)}, u32[]{:S(2)}) %copy-start.2) | copy-done | bytes 24600
  4.1 0.0 copy-start.3
  4.1 0.8 %copy-done.3 = bf16[128,96]{1,0:T(8,128)(2,1)S(1)} copy-done((bf16[128,96]{1,0:T(8,128)(2,1)S(1)}, bf16[128,96]{1,0:T(8,128)(2,1)}, u32[]{:S(2)}) %copy-start.3) | copy-done | bytes 24600
  4.9 0.0 copy-start.4
  4.9 0.8 %copy-done.4 = bf16[128,128]{1,0:T(8,128)(2,1)S(1)} copy-done((bf16[128,128]{1,0:T(8,128)(2,1)S(1)}, bf16[128,128]{1,0:T(8,128)(2,1)}, u32[]{:S(2)}) %copy-start.4) | copy-done | bytes 32792
  5.6 46.5 %shard_map.77 = (f32[512,128]{1,0:T(8,128)S(1)}, f32[1,4]{1,0:T(1,128)S(1)}) custom-call(s32[4]{0:T(128)S(1)} %copy-done.5, f32[2048,128]{1,0:T(8,128)S(1)} %bitcast.2, bf16[256,128]{1,0:T(8,128)(2,1)S(1)} %copy-done.1, bf16[128,128]{1,0:T(8,128)(2,1)S(1)} %copy-done.4, bf16[128,96]{1,0:T(8,128)(2,1)S(1)} %copy-done.3, bf16[64,192]{1,0:T(8,128)(2,1)S(1)} %copy-done.2), custom_call_target="tpu_custom_call" | custom-call | tf_op jit(solution)/shard_map/pallas_call | solution.py:598
  52.2 0.7 %copy.10 = f32[1,65536]{1,0:T(1,128)} copy(f32[1,65536]{1,0:T(1,128)S(1)} %bitcast.3) | data formatting | bytes 524288
  52.9 0.5 copy.11
Async XLA Ops:
  0.6 0.7 %copy-start.5 = (s32[4]{0:T(128)S(1)}, s32[4]{0:T(128)}, u32[]{:S(2)}) copy-start(s32[4]{0:T(128)} %offsets_ref.1) | copy-start | bytes 52
  1.3 1.2 %copy-start = (f32[1,262144]{1,0:T(1,128)S(1)}, f32[1,262144]{1,0:T(1,128)}, u32[]{:S(2)}) copy-start(f32[1,262144]{1,0:T(1,128)} %param.6) | copy-start | bytes 3145732
  2.5 0.8 %copy-start.1 = (bf16[256,128]{1,0:T(8,128)(2,1)S(1)}, bf16[256,128]{1,0:T(8,128)(2,1)}, u32[]{:S(2)}) copy-start(bf16[256,128]{1,0:T(8,128)(2,1)} %constant.8.clone.main_ref) | copy-start | bytes 196612
  3.4 0.8 %copy-start.2 = (bf16[64,192]{1,0:T(8,128)(2,1)S(1)}, bf16[64,192]{1,0:T(8,128)(2,1)}, u32[]{:S(2)}) copy-start(bf16[64,192]{1,0:T(8,128)(2,1)} %constant.11.clone.first_ref) | copy-start | bytes 73732
  4.1 0.8 %copy-start.3 = (bf16[128,96]{1,0:T(8,128)(2,1)S(1)}, bf16[128,96]{1,0:T(8,128)(2,1)}, u32[]{:S(2)}) copy-start(bf16[128,96]{1,0:T(8,128)(2,1)} %constant.10.clone.middle_ref) | copy-start | bytes 73732
  4.9 0.8 %copy-start.4 = (bf16[128,128]{1,0:T(8,128)(2,1)S(1)}, bf16[128,128]{1,0:T(8,128)(2,1)}, u32[]{:S(2)}) copy-start(bf16[128,128]{1,0:T(8,128)(2,1)} %constant.9.clone.low_ref) | copy-start | bytes 98308
